TPU v7x, 32 devices: a whole 2x2x4 slice. The times are simulated.
32 devices in a mesh: grp: 2 (over y), gx: 4 (over z), gy: 2 (over x), gz: 2 (over core).
Axes of the slice: x: 2, y: 2, z: 4, core: 2. Of those that a mesh axis runs over, the one named last changes fastest.
Arguments:
- feats: bfloat16 [16, 128, 48, 256], P(None, ('grp', 'gx'), 'gy', 'gz'), parts along dimension 1, may hold values from -6 to 6
- kernel: bfloat16 [27, 16, 16], replicated, may hold values from -0.3125 to 0.3125
- proj: float32 [16], replicated, may hold values from -1.5 to 1.5
- perm: float32 [128, 48, 256], P(('grp', 'gx'), 'gy', 'gz'), parts along dimension 0, may hold values from 0.1 to 1
- source: float32 [128, 48, 256], P(('grp', 'gx'), 'gy', 'gz'), parts along dimension 0, may hold values from -6 to 6
Outputs:
- residual: float32 [128, 48, 256], P(('grp', 'gx'), 'gy', 'gz'), parts along dimension 0
- kernel_grad: float32 [54, 16, 16], P('grp'), parts along dimension 0
- proj_grad: float32 [32], P('grp'), parts along dimension 0
- feats_grad: bfloat16 [16, 128, 48, 256], P(None, ('grp', 'gx'), 'gy', 'gz'), parts along dimension 1
There are 2 independent parts, one for each index of `grp`. A program takes and returns all parts, laid end to end along the dimension named above; an argument that names none is the same for every part. Nothing has to cross between parts.
All inputs are finite; a program needn't handle non-finite values.
Results may differ from a plain program's by a relative error of at most 0.013.
Values may be sent and summed in bfloat16 or wider, within the bound.
No kernel may reach another device: no remote copies, remote signals or barrier semaphores. Data moves between devices by JAX's collectives and lax.ppermute only.
A program may use at most 128 MiB of HBM per device.

v0:
```python
import jax
import jax.numpy as jnp
from jax import lax
from jax.experimental import pallas as pl
from jax.experimental.pallas import tpu as pltpu
from jax.sharding import PartitionSpec as P

GROUP = ("gx", "gy", "gz")
HALO = 4
F32 = jnp.float32
BF16 = jnp.bfloat16


def routes(sizes, target):
    nx, ny, nz = sizes
    pairs = []
    for x in range(nx):
        for y in range(ny):
            for z in range(nz):
                tx, ty, tz = target(x, y, z)
                if 0 <= tx < nx and 0 <= ty < ny:
                    pairs.append(((x * ny + y) * nz + z, (tx * ny + ty) * nz + tz))
    return pairs


def pack_kernel(sides, flags, feats, perm, source, own, swap, near, far, *edges):
    half = flags[0]
    channels, planes, rows, lanes = feats.shape
    count = channels * rows
    row_id = lax.broadcasted_iota(jnp.int32, (count, count), 0)
    col_id = lax.broadcasted_iota(jnp.int32, (count, count), 1)
    order = (row_id % channels) * rows + row_id // channels
    permute = jnp.where(order == col_id, 1.0, 0.0).astype(BF16)
    wide = planes * 3 // 4

    def put(ref, index, limit, value):
        @pl.when((index >= 0) & (index < limit))
        def _():
            ref[index] = value

    def pair_step(pair, carry):
        x0 = pair * 2
        parts = [feats[:, x0 + j].astype(F32).reshape(count, lanes).astype(BF16) for j in range(2)]
        moved = jnp.dot(permute, jnp.concatenate(parts, axis=1), preferred_element_type=F32)
        for j in range(2):
            x = x0 + j
            cells = moved[:, j * lanes : (j + 1) * lanes]
            coefficient = perm[x]
            term = source[x]
            coefficient_hi = coefficient.astype(BF16).astype(F32)
            term_hi = term.astype(BF16).astype(F32)
            extra = [coefficient_hi, coefficient - coefficient_hi, term_hi, term - term_hi]
            plane = jnp.concatenate([cells] + extra, axis=0).astype(BF16)
            own[x] = plane
            put(swap, x - HALO * (1 - half), wide, plane)
            high = x - (planes - HALO)
            put(near, jnp.where(half == 0, high, x), HALO, plane)
            put(far, jnp.where(half == 0, x, high), HALO, plane)
            pieces = []
            for low_side in (True, False):
                start = 0 if low_side else rows - HALO
                pieces.append(
                    jnp.concatenate(
                        [cells[start * channels : (start + HALO) * channels]]
                        + [e[start : start + HALO] for e in extra],
                        axis=0,
                    )
                )
            if sides == 1:
                pieces = [jnp.where(flags[1] == 0, pieces[1], pieces[0])]
            else:
                pieces = [pieces[1], pieces[0]]
            for side in range(sides):
                piece = pieces[side].astype(BF16)
                e_same, e_cross, e_near, e_far = edges[4 * side : 4 * side + 4]
                put(e_same, x - HALO * half, wide, piece)
                put(e_cross, x - HALO * (1 - half), wide, piece)
                put(e_near, jnp.where(half == 0, high, x), HALO, piece)
                put(e_far, jnp.where(half == 0, x, high), HALO, piece)
        return carry

    lax.fori_loop(0, planes // 2, pair_step, 0)


def pack(feats, perm, source, flags, sides):
    channels, planes, rows, lanes = feats.shape
    full = rows * (channels + 4)
    edge = HALO * (channels + 4)
    wide = planes * 3 // 4
    shapes = [(planes, full), (wide, full), (HALO, full), (HALO, full)]
    shapes += [(wide, edge), (wide, edge), (HALO, edge), (HALO, edge)] * sides
    return pl.pallas_call(
        lambda *refs: pack_kernel(sides, *refs),
        out_shape=[jax.ShapeDtypeStruct(s + (lanes,), BF16) for s in shapes],
        in_specs=[pl.BlockSpec(memory_space=pltpu.SMEM)] + [pl.BlockSpec(memory_space=pltpu.VMEM)] * 3,
        out_specs=[pl.BlockSpec(memory_space=pltpu.VMEM)] * len(shapes),
        name="pack",
    )(flags, feats, perm, source)


def lane_shift(value, offset):
    size = value.shape[1]
    lane = lax.broadcasted_iota(jnp.int32, value.shape, 1)
    if offset < 0:
        return jnp.where(lane == 0, 0.0, pltpu.roll(value, 1, 1))
    return jnp.where(lane == size - 1, 0.0, pltpu.roll(value, size - 1, 1))


def sigmoid(value):
    return 0.5 * jnp.tanh(0.5 * value) + 0.5


def main_kernel(
    channels, rows, flags,
    own, swap, near, far, lo_same, lo_cross, lo_near, lo_far, hi_same, hi_cross, hi_near, hi_far,
    weights_fwd, weights_bwd, proj_rows,
    res_own, res_send, fg_own, fg_send, grads,
    fwide, gwide, pre_ref, coef, src, vfield, face_x, face_y, face_z, rfield, afield,
    acc_a, acc_b, kacc, pacc,
):
    half, has_ylo, has_yhi, has_xlo, has_xhi = (flags[i] for i in (0, 2, 3, 4, 5))
    lanes = own.shape[2]
    zsize = 2 * lanes
    ext_y = rows + 2 * HALO
    wide = swap.shape[0]
    ext_x = wide + HALO
    inner = ext_x - 2 * HALO
    taps = 3 * channels
    window = 10 * taps
    block = 8 * channels
    yblocks = ext_y // 8
    oblocks = rows // 8
    cell_rows = rows * channels
    edge_rows = HALO * channels

    def spread(ref, index, value, y0):
        n = value.shape[0] // channels
        for tap, shifted in enumerate((lane_shift(value, -1), value, lane_shift(value, 1))):
            for side in range(2):
                piece = shifted[:, side * lanes : (side + 1) * lanes].astype(BF16)
                ref[index, side, pl.ds(y0, n), tap * channels : (tap + 1) * channels, :] = piece.reshape(
                    n, channels, lanes
                )

    def joined(mine, other):
        a = mine.astype(F32)
        b = other.astype(F32)
        return jnp.concatenate([jnp.where(half == 0, a, b), jnp.where(half == 0, b, a)], axis=1)

    def fill(e, main_mine, main_other, lo_mine, lo_other, hi_mine, hi_other):
        centre = joined(main_mine, main_other)
        low = joined(lo_mine, lo_other)
        high = joined(hi_mine, hi_other)
        spread(fwide, e, jnp.where(has_ylo == 1, low[:edge_rows], 0.0), 1)
        spread(fwide, e, centre[:cell_rows], 1 + HALO)
        spread(fwide, e, jnp.where(has_yhi == 1, high[:edge_rows], 0.0), 1 + HALO + rows)
        zero = jnp.zeros((1, taps, lanes), BF16)
        for side in range(2):
            fwide[e, side, 0:1] = zero
            fwide[e, side, ext_y + 1 : ext_y + 2] = zero

        def full(kind):
            def at(value, base, n):
                start = base + kind * n
                return value[start : start + n] + value[start + n : start + 2 * n]

            mid = at(centre, cell_rows, rows)
            first = jnp.where(has_ylo == 1, at(low, edge_rows, HALO), mid[0:1])
            last = jnp.where(has_yhi == 1, at(high, edge_rows, HALO), mid[rows - 1 : rows])
            return jnp.concatenate([first, mid, last], axis=0)

        coef[e] = full(0)
        src[e] = full(2)

    def fill_wide(j, carry):
        fill(j + HALO * (1 - half), own[HALO * half + j], swap[j], lo_same[j], lo_cross[j], hi_same[j], hi_cross[j])
        return carry

    lax.fori_loop(0, wide, fill_wide, 0)

    def fill_far(j, carry):
        fill(j + wide * half, near[j], far[j], lo_near[j], lo_far[j], hi_near[j], hi_far[j])
        return carry

    lax.fori_loop(0, HALO, fill_far, 0)

    @pl.when(has_xlo == 0)
    def _():
        for e in range(HALO):
            coef[e] = coef[HALO]

    @pl.when(has_xhi == 0)
    def _():
        for e in range(ext_x - HALO, ext_x):
            coef[e] = coef[ext_x - HALO - 1]

    proj_block = jnp.concatenate([proj_rows[...]] * 8, axis=0)
    row_index = lax.broadcasted_iota(jnp.int32, (ext_y, zsize), 0)
    y_inside = ((row_index >= HALO) | (has_ylo == 1)) & ((row_index < HALO + rows) | (has_yhi == 1))
    lane_index = lax.broadcasted_iota(jnp.int32, (ext_y, zsize), 1)

    def masked(e, value):
        x_inside = ((e >= HALO) | (has_xlo == 1)) & ((e < ext_x - HALO) | (has_xhi == 1))
        return jnp.where(y_inside & x_inside, value, 0.0)

    def taps_of(ref, e, y0):
        return jnp.concatenate([ref[e, s, pl.ds(y0, 10)].reshape(window, lanes) for s in range(2)], axis=1)

    for yb in range(yblocks):

        def product(e):
            return jnp.dot(weights_fwd[...], taps_of(fwide, e, 8 * yb), preferred_element_type=F32)

        first = product(0)
        second = product(1)
        acc_b[0] = first[:block] + second[block : 2 * block]
        acc_a[0] = second[:block]

        def conv_step(e, carry):
            result = product(e)
            pre = acc_b[0] + result[2 * block :]
            acc_b[0] = acc_a[0] + result[block : 2 * block]
            acc_a[0] = result[:block]
            pre_ref[e - 2, yb] = pre
            active = pre * sigmoid(pre) * proj_block
            vfield[e - 2, 8 * yb : 8 * yb + 8, :] = jnp.sum(active.reshape(8, channels, zsize), axis=1)
            return carry

        lax.fori_loop(2, ext_x, conv_step, 0)

    def face(a, b):
        return 2.0 * a * b / (a + b)

    def face_step(e, carry):
        centre = coef[e]
        face_x[e] = face(centre, coef[jnp.minimum(e + 1, ext_x - 1)])
        face_y[e] = face(centre, pltpu.roll(centre, ext_y - 1, 0))
        face_z[e] = jnp.where(lane_index == zsize - 1, centre, face(centre, pltpu.roll(centre, zsize - 1, 1)))
        return carry

    lax.fori_loop(0, ext_x, face_step, 0)

    def operator(e, below, centre, above):
        flux_y = face_y[e] * (centre - pltpu.roll(centre, ext_y - 1, 0))
        flux_z = face_z[e] * (centre - lane_shift(centre, 1))
        left_z = jnp.where(lane_index == 0, -coef[e] * centre, pltpu.roll(flux_z, 1, 1))
        total = face_x[e] * (centre - above) + face_x[e - 1] * (centre - below)
        return total + (flux_y - pltpu.roll(flux_y, 1, 0)) + (flux_z - left_z)

    def mask_step(i, carry):
        vfield[i] = masked(i + 1, vfield[i])
        return carry

    lax.fori_loop(0, ext_x - 2, mask_step, 0)

    def residual_step(i, carry):
        value = operator(i + 2, vfield[i], vfield[i + 1], vfield[i + 2]) - src[i + 2]
        rfield[i] = masked(i + 2, value)
        return carry

    lax.fori_loop(0, ext_x - 4, residual_step, 0)

    def residual_out(x, carry):
        value = rfield[x + 2][HALO : HALO + rows]
        low = value[:, :lanes]
        high = value[:, lanes:]
        res_own[x] = jnp.where(half == 0, low, high)
        res_send[x] = jnp.where(half == 0, high, low)
        return carry

    lax.fori_loop(0, inner, residual_out, 0)

    def adjoint_step(i, carry):
        afield[i] = masked(i + 3, operator(i + 3, rfield[i], rfield[i + 1], rfield[i + 2]))
        return carry

    lax.fori_loop(0, ext_x - 6, adjoint_step, 0)

    pacc[...] = jnp.zeros(pacc.shape, F32)

    def grad_step(i, carry):
        for yb in range(yblocks):
            pre = pre_ref[i + 2, yb]
            sig = sigmoid(pre)
            near_adj = afield[i, 8 * yb : 8 * yb + 8, :]
            adj = jnp.broadcast_to(near_adj[:, None, :], (8, channels, zsize)).reshape(block, zsize)
            slope = sig * (1.0 + pre * (1.0 - sig))
            value = (adj * proj_block * slope).astype(BF16).astype(F32)
            spread(gwide, i, value, 8 * yb + 1)
            lo = max(HALO - 8 * yb, 0)
            hi = min(HALO + rows - 8 * yb, 8)
            term = (adj * (pre * sig))[lo * channels : hi * channels]
            total = term[:channels]
            for y in range(1, hi - lo):
                total = total + term[y * channels : (y + 1) * channels]

            @pl.when((i >= 1) & (i <= inner))
            def _():
                pacc[...] += total

        return carry

    lax.fori_loop(0, ext_x - 6, grad_step, 0)

    def back_product(i, b):
        return jnp.dot(weights_bwd[...], taps_of(gwide, i, HALO + 8 * b), preferred_element_type=F32)

    for b in range(oblocks):
        first = back_product(0, b)
        second = back_product(1, b)
        acc_b[b] = first[:block] + second[block : 2 * block]
        acc_a[b] = second[:block]

    def back_step(i, carry):
        parts = []
        for b in range(oblocks):
            result = back_product(i, b)
            parts.append((acc_b[b] + result[2 * block :]).reshape(channels, 8, zsize))
            acc_b[b] = acc_a[b] + result[block : 2 * block]
            acc_a[b] = result[:block]
        value = jnp.concatenate(parts, axis=1)
        low = value[:, :, :lanes]
        high = value[:, :, lanes:]
        fg_own[:, i - 2] = jnp.where(half == 0, low, high).astype(BF16)
        fg_send[:, i - 2] = jnp.where(half == 0, high, low).astype(BF16)
        return carry

    lax.fori_loop(2, inner + 2, back_step, 0)

    kacc[...] = jnp.zeros(kacc.shape, F32)

    def kernel_step(x, carry):
        for dx in range(3):
            total = kacc[dx]
            for b in range(oblocks):
                y0 = HALO + 1 + 8 * b
                pieces = [
                    gwide[x + 1, s, y0 : y0 + 8, channels : 2 * channels, :].reshape(block, lanes) for s in range(2)
                ]
                total = total + lax.dot_general(
                    taps_of(fwide, x + HALO - 1 + dx, HALO + 8 * b),
                    jnp.concatenate(pieces, axis=1),
                    (((1,), (1,)), ((), ())),
                    preferred_element_type=F32,
                )
            kacc[dx] = total
        return carry

    lax.fori_loop(0, inner, kernel_step, 0)

    lane_group = lax.broadcasted_iota(jnp.int32, (3 * taps, block), 1) // channels
    sub_row = lax.broadcasted_iota(jnp.int32, (3 * taps, block), 0) % (block // channels)
    per_dx = 3 * taps * channels // block
    for dx in range(3):
        picked = jnp.zeros((3 * taps, block), F32)
        for y in range(8):
            picked = jnp.where(lane_group == y, kacc[dx, y * taps : y * taps + 3 * taps], picked)
        step = channels
        while step < block:
            picked = picked + pltpu.roll(picked, step, 1)
            step *= 2
        packed = jnp.where(lane_group == sub_row, picked, 0.0).reshape(per_dx, block // channels, block)
        grads[dx * per_dx : (dx + 1) * per_dx, :] = jnp.sum(packed, axis=1)
    per_channel = jnp.sum(pacc[...], axis=1, keepdims=True)
    chan_row = lax.broadcasted_iota(jnp.int32, (channels, block), 0)
    chan_lane = lax.broadcasted_iota(jnp.int32, (channels, block), 1)
    flat = jnp.sum(jnp.where(chan_row == chan_lane, per_channel, 0.0), axis=0, keepdims=True)
    grads[3 * per_dx :, :] = jnp.broadcast_to(flat, (grads.shape[0] - 3 * per_dx, block))


def main(channels, rows, flags, tensors, weights_fwd, weights_bwd, proj_rows):
    own, swap = tensors[0], tensors[1]
    lanes = own.shape[2]
    zsize = 2 * lanes
    wide = swap.shape[0]
    ext_x = wide + HALO
    ext_y = rows + 2 * HALO
    inner = ext_x - 2 * HALO
    taps = 3 * channels
    block = 8 * channels
    oblocks = rows // 8
    grad_rows = 27 * channels * channels // block
    out_rows = -(-(grad_rows + 1) // 8) * 8
    vmem = pl.BlockSpec(memory_space=pltpu.VMEM)
    plane = (ext_y, zsize)
    return pl.pallas_call(
        lambda *refs: main_kernel(channels, rows, *refs),
        out_shape=[
            jax.ShapeDtypeStruct((inner, rows, lanes), F32),
            jax.ShapeDtypeStruct((inner, rows, lanes), F32),
            jax.ShapeDtypeStruct((channels, inner, rows, lanes), BF16),
            jax.ShapeDtypeStruct((channels, inner, rows, lanes), BF16),
            jax.ShapeDtypeStruct((out_rows, block), F32),
        ],
        in_specs=[pl.BlockSpec(memory_space=pltpu.SMEM)] + [vmem] * (len(tensors) + 3),
        out_specs=[vmem] * 5,
        scratch_shapes=[
            pltpu.VMEM((ext_x, 2, ext_y + 2, taps, lanes), BF16),
            pltpu.VMEM((ext_x - 6, 2, ext_y + 2, taps, lanes), BF16),
            pltpu.VMEM((ext_x - 2, ext_y // 8, block, zsize), F32),
            pltpu.VMEM((ext_x,) + plane, F32),
            pltpu.VMEM((ext_x,) + plane, F32),
            pltpu.VMEM((ext_x - 2,) + plane, F32),
            pltpu.VMEM((ext_x,) + plane, F32),
            pltpu.VMEM((ext_x,) + plane, F32),
            pltpu.VMEM((ext_x,) + plane, F32),
            pltpu.VMEM((ext_x - 4,) + plane, F32),
            pltpu.VMEM((ext_x - 6,) + plane, F32),
            pltpu.VMEM((oblocks, block, zsize), F32),
            pltpu.VMEM((oblocks, block, zsize), F32),
            pltpu.VMEM((3, 10 * taps, block), F32),
            pltpu.VMEM((channels, zsize), F32),
        ],
        compiler_params=pltpu.CompilerParams(vmem_limit_bytes=58 * 1024 * 1024),
        name="step",
    )(flags, *tensors, weights_fwd, weights_bwd, proj_rows)


def band(base, y):
    rest = 7 * base.shape[-1] // 3
    shift = y * base.shape[-1] // 3
    return jnp.pad(base, ((0, 0), (0, 0), (shift, rest - shift)))


def banded_weights(kernel):
    channels = kernel.shape[1]
    grid = kernel.reshape(3, 9, channels, channels)
    base = grid.transpose(0, 2, 1, 3).reshape(3, channels, 9 * channels)
    forward = jnp.stack([band(base, y) for y in range(8)], axis=1)
    flipped = grid[::-1, ::-1].transpose(0, 3, 1, 2).reshape(3, channels, 9 * channels)
    backward = jnp.stack([band(flipped, y) for y in range(8)], axis=2)
    return forward.reshape(24 * channels, -1), backward.reshape(24 * channels, -1)


def local(feats, kernel, proj, perm, source):
    channels, planes, rows, lanes = feats.shape
    sizes = tuple(lax.axis_size(a) for a in GROUP)
    nx, ny, _ = sizes
    gx, gy, half = (lax.axis_index(a) for a in GROUP)
    has_xlo = (gx > 0) | (half == 1)
    has_xhi = (gx < nx - 1) | (half == 0)
    flags = jnp.stack([half, gy, gy > 0, gy < ny - 1, has_xlo, has_xhi]).astype(jnp.int32)
    sides = 1 if ny == 2 else 2

    def send(value, target):
        return lax.ppermute(value, GROUP, routes(sizes, target))

    def step_x(x, z):
        return x + 1 if z == 0 else x - 1

    def step_far(x, z):
        return x - 1 if z == 0 else x + 1

    own, swap, near, far, *edges = pack(feats, perm, source, flags, sides)
    got = [own]
    got.append(send(swap, lambda x, y, z: (x, y, 1 - z)))
    got.append(send(near, lambda x, y, z: (step_x(x, z), y, z)))
    got.append(send(far, lambda x, y, z: (step_far(x, z), y, 1 - z)))
    received = []
    for side in range(sides):
        same, cross, e_near, e_far = edges[4 * side : 4 * side + 4]

        def step_y(y, side=side):
            if sides == 1:
                return 1 - y
            return y + 1 if side == 0 else y - 1

        received.append(
            [
                send(same, lambda x, y, z: (x, step_y(y), z)),
                send(cross, lambda x, y, z: (x, step_y(y), 1 - z)),
                send(e_near, lambda x, y, z: (step_x(x, z), step_y(y), z)),
                send(e_far, lambda x, y, z: (step_far(x, z), step_y(y), 1 - z)),
            ]
        )
    got += received[0] + received[-1]
    weights_fwd, weights_bwd = banded_weights(kernel)
    proj_rows = jnp.broadcast_to(proj[:, None], (channels, 2 * lanes))
    res_own, res_send, fg_own, fg_send, grads = main(
        channels, rows, flags, got, weights_fwd, weights_bwd, proj_rows
    )

    def partner(value):
        return send(value, lambda x, y, z: (x, y, 1 - z))

    res_got = partner(res_send)
    fg_got = partner(fg_send)

    def ordered(mine, other, axis):
        return jnp.where(
            half == 0, jnp.concatenate([mine, other], axis), jnp.concatenate([other, mine], axis)
        )

    residual = ordered(res_own, res_got, 0)
    feats_grad = ordered(fg_own, fg_got, 1)
    grads = grads + partner(grads)
    for axis in ("gy", "gx"):
        count = lax.axis_size(axis)
        step = 1
        while step < count:
            grads = grads + lax.ppermute(grads, axis, [(i, i ^ step) for i in range(count)])
            step *= 2
    grad_rows = 27 * channels * channels // grads.shape[1]
    kernel_grad = grads[:grad_rows].reshape(27, channels, channels).transpose(0, 2, 1)
    proj_grad = grads[grad_rows, :channels]
    return (residual, kernel_grad, proj_grad, feats_grad)


def solution(mesh):
    in_specs = (
        P(None, ("grp", "gx"), "gy", "gz"),
        P(),
        P(),
        P(("grp", "gx"), "gy", "gz"),
        P(("grp", "gx"), "gy", "gz"),
    )
    out_specs = (
        P(("grp", "gx"), "gy", "gz"),
        P("grp", None, None),
        P("grp"),
        P(None, ("grp", "gx"), "gy", "gz"),
    )
    return jax.shard_map(local, mesh=mesh, in_specs=in_specs, out_specs=out_specs, check_vma=False)
```

profile of v0, /device:TPU:0, one launch (start us, length us, event | category | flops | bytes accessed | tf_op | source)
XLA Modules:
  0.0 112.2 jit_solution(12804486672000474904)
XLA Ops:
  0.7 0.6 stack.97.refs_0_
  1.3 6.8 %pack.1 = (bf16[16,480,128]{2,1,0:T(8,128)(2,1)}, bf16[12,480,128]{2,1,0:T(8,128)(2,1)}, bf16[4,480,128]{2,1,0:T(8,128)(2,1)}, bf16[4,480,128]{2,1,0:T(8,128)(2,...) custom-call(s32[6]{0:T(128)} %stack.97.refs_0_, ...), custom_call_target="tpu_custom_call" | custom-call | tf_op jit(solution)/shard_map/pack/pallas_call | solution.py:92
  8.6 5.4 %collective-permute-start.5 = (bf16[4,80,128]{2,1,0:T(8,128)(2,1)}, bf16[4,80,128]{2,1,0:T(8,128)(2,1)S(1)}, u32[]{:S(2)}, u32[]{:S(2)}) collective-permute-start(bf16[4,80,128]{2,1,0:T(8,128)(2,1)} %get-tuple-element.23), channel_id=1, source_target_pairs={{0,6},{2,4},{4,10},{5,3},{6,8},{7,1},{8,14},{9,7},{10,12},{11,5},{... | collective-permute-start | bytes 245768 | tf_op jit(solution)/shard_map/ppermute | solution.py:446
  14.0 1.3 %collective-permute-start.6 = (bf16[4,80,128]{2,1,0:T(8,128)(2,1)}, bf16[4,80,128]{2,1,0:T(8,128)(2,1)}, u32[]{:S(2)}, u32[]{:S(2)}) collective-permute-start(bf16[4,80,128]{2,1,0:T(8,128)(2,1)} %get-tuple-element.24), channel_id=1, source_target_pairs={{1,6},{3,4},{4,3},{5,10},{6,1},{7,8},{8,7},{9,14},{10,5},{11,12},{... | collective-permute-start | bytes 245768 | tf_op jit(solution)/shard_map/ppermute | solution.py:446
  15.2 4.9 %collective-permute-start.1 = (bf16[4,480,128]{2,1,0:T(8,128)(2,1)}, bf16[4,480,128]{2,1,0:T(8,128)(2,1)}, u32[]{:S(2)}, u32[]{:S(2)}) collective-permute-start(bf16[4,480,128]{2,1,0:T(8,128)(2,1)} %get-tuple-element.19), channel_id=1, source_target_pairs={{0,4},{2,6},{4,8},{5,1},{6,10},{7,3},{8,12},{9,5},{10,14},{11,7},{... | collective-permute-start | bytes 1474568 | tf_op jit(solution)/shard_map/ppermute | solution.py:446
  20.2 1.4 %collective-permute-start.2 = (bf16[4,480,128]{2,1,0:T(8,128)(2,1)}, bf16[4,480,128]{2,1,0:T(8,128)(2,1)}, u32[]{:S(2)}, u32[]{:S(2)}) collective-permute-start(bf16[4,480,128]{2,1,0:T(8,128)(2,1)} %get-tuple-element.20), channel_id=1, source_target_pairs={{1,4},{3,6},{4,1},{5,8},{6,3},{7,10},{8,5},{9,12},{10,7},{11,14},{... | collective-permute-start | bytes 1474568 | tf_op jit(solution)/shard_map/ppermute | solution.py:446
  22.1 1.3 %pad_bitcast_fusion.8 = (bf16[3,1,16,480]{2,3,0,1:T(8,128)(2,1)}, bf16[3,1,16,480]{2,3,0,1:T(8,128)(2,1)S(1)}, bf16[3,1,16,480]{2,3,0,1:T(8,128)(2,1)}, bf16[3,1...) fusion(bf16[3,16,144]{1,2,0:T(8,128)(2,1)S(1)} %bitcast.56), kind=kLoop, calls=%fused_computation.9 | loop fusion | bytes 382464 | tf_op jit(solution)/shard_map/stack | solution.py:429
  23.3 0.8 copy.38
  24.6 0.7 constant_dynamic-update-slice_fusion.7
  25.2 0.6 constant_dynamic-update-slice_fusion.6
  25.8 0.6 constant_dynamic-update-slice_fusion.5
  26.8 0.6 constant_dynamic-update-slice_fusion.4
  27.5 1.1 copy.40
  28.6 1.1 %copy.39 = bf16[3,1,16,480]{3,2,1,0:T(8,128)(2,1)S(1)} copy(bf16[3,1,16,480]{2,3,0,1:T(8,128)(2,1)} %get-tuple-element.49) | data formatting | bytes 92160 | tf_op jit(solution)/shard_map/stack | solution.py:429
  29.7 0.6 constant_dynamic-update-slice_fusion.3
  30.9 2.2 %collective-permute-start.4 = (bf16[12,80,128]{2,1,0:T(8,128)(2,1)}, bf16[12,80,128]{2,1,0:T(8,128)(2,1)}, u32[]{:S(2)}, u32[]{:S(2)}) collective-permute-start(bf16[12,80,128]{2,1,0:T(8,128)(2,1)} %get-tuple-element.22), channel_id=1, source_target_pairs={{0,3},{1,2},{2,1},{3,0},{4,7},{5,6},{6,5},{7,4},{8,11},{9,10},{10,... | collective-permute-start | bytes 737288 | tf_op jit(solution)/shard_map/ppermute | solution.py:446
  33.1 0.6 constant_dynamic-update-slice_fusion.2
  36.3 2.1 %stack.115 = bf16[3,16,8,480]{3,2,1,0:T(8,128)(2,1)} concatenate(bf16[3,16,1,480]{3,2,1,0:T(2,128)(2,1)S(1)} %copy.44, bf16[3,16,1,480]{3,2,1,0:T(2,128)(2,1)S(1)} %copy.45, bf16[3,16,1,480]{3,2,1,0:T(2,128)(2,1)S(1)} %copy.46, bf16[3,16,1,480]{3,2,1,0:T(2,128)(2,1)S(1)} %copy.47, bf16[3,16,1,480]{3,2,1,0:T(2,128)(2,1)S(1)} %copy.48, bf16[3,16,1,480]{3,2,1,0:T(2,128)(2,1)S(1)} %copy.49, ...), dimensions={2} | concatenate | bytes 737280 | tf_op jit(solution)/shard_map/stack | solution.py:431
  38.4 0.6 constant_dynamic-update-slice_fusion.1
  39.7 5.1 %collective-permute-done.4.refs_6_.refs_10_ = bf16[12,80,128]{2,1,0:T(8,128)(2,1)} collective-permute-done((bf16[12,80,128]{2,1,0:T(8,128)(2,1)}, bf16[12,80,128]{2,1,0:T(8,128)(2,1)}, u32[]{:S(2)}, u32[]{:S(2)}) %collective-permute-start.4) | collective-permute-done | bytes 245792 | tf_op jit(solution)/shard_map/ppermute | solution.py:446
  44.8 0.7 broadcast_in_dim.2.refs_15_
  45.5 47.9 %step.1 = (f32[8,24,128]{2,1,0:T(8,128)}, f32[8,24,128]{2,1,0:T(8,128)}, bf16[16,8,24,128]{3,2,1,0:T(8,128)(2,1)}, bf16[16,8,24,128]{3,2,1,0:T(8,128)(2,1)}, f32[56,128]{1,0:T(8,128)}) custom-call(s32[6]{0:T(128)} %stack.97.refs_0_, bf16[16,480,128]{2,1,0:T(8,128)(2,1)} %get-tuple-element.17.refs_1_, bf16[12,480,128]{2,1,0:T(8,128)(2,1)} %collective-permute-done.refs_2_, ...), custom_call_target="tpu_custom_call" | custom-call | tf_op jit(solution)/shard_map/step/pallas_call | solution.py:386
  94.0 2.1 %collective-permute-done.8 = f32[56,128]{1,0:T(8,128)S(1)} collective-permute-done((f32[56,128]{1,0:T(8,128)}, f32[56,128]{1,0:T(8,128)S(1)}, u32[]{:S(2)}, u32[]{:S(2)}) %collective-permute-start.8) | collective-permute-done | bytes 28704 | tf_op jit(solution)/shard_map/ppermute | solution.py:446
  96.1 0.8 add.44
  97.4 3.3 %collective-permute-done.9 = f32[56,128]{1,0:T(8,128)S(1)} collective-permute-done((f32[56,128]{1,0:T(8,128)S(1)}, f32[56,128]{1,0:T(8,128)S(1)}, u32[]{:S(2)}, u32[]{:S(2)}) %collective-permute-start.9) | collective-permute-done | bytes 28704 | tf_op jit(solution)/shard_map/ppermute | solution.py:501
  100.8 0.9 collective-permute-start.10
  101.7 3.0 %collective-permute-done.10 = f32[56,128]{1,0:T(8,128)S(1)} collective-permute-done((f32[56,128]{1,0:T(8,128)S(1)}, f32[56,128]{1,0:T(8,128)S(1)}, u32[]{:S(2)}, u32[]{:S(2)}) %collective-permute-start.10) | collective-permute-done | bytes 28704 | tf_op jit(solution)/shard_map/ppermute | solution.py:501
  104.6 1.0 collective-permute-start.11
  105.6 1.7 %maximum_select_fusion.1 = f32[16,24,128]{2,1,0:T(8,128)} fusion(f32[8,24,128]{2,1,0:T(8,128)S(1)} %collective-permute-done.7, f32[8,24,128]{2,1,0:T(8,128)} %get-tuple-element.25, pred[]{:T(512)S(6)} %eq.8), kind=kLoop, calls=%fused_computation.17 | loop fusion | flops 147456 | bytes 393217 | tf_op jit(solution)/shard_map/jit(_where)/select_n | solution.py:490
  107.3 2.1 %collective-permute-done.11 = f32[56,128]{1,0:T(8,128)S(1)} collective-permute-done((f32[56,128]{1,0:T(8,128)S(1)}, f32[56,128]{1,0:T(8,128)S(1)}, u32[]{:S(2)}, u32[]{:S(2)}) %collective-permute-start.11) | collective-permute-done | bytes 28704 | tf_op jit(solution)/shard_map/ppermute | solution.py:501
  109.5 0.8 copy.52
  110.9 1.3 %maximum_select_fusion = bf16[16,16,24,128]{3,2,1,0:T(8,128)(2,1)} fusion(bf16[16,8,24,128]{3,2,1,0:T(8,128)(2,1)S(1)} %collective-permute-done.12, bf16[16,8,24,128]{3,2,1,0:T(8,128)(2,1)S(1)} %copy-done.1, pred[]{:T(512)S(6)} %eq.8), kind=kLoop, calls=%fused_computation | loop fusion | flops 2359296 | bytes 3145729 | tf_op jit(solution)/shard_map/jit(_where)/select_n | solution.py:490
  (49 shorter events, 7.3 us)
Async XLA Ops:
  0.6 21.0 %copy-start.3 = (bf16[27,16,16]{0,2,1:T(8,128)(2,1)S(1)}, bf16[27,16,16]{0,2,1:T(8,128)(2,1)}, u32[]{:S(2)}) copy-start(bf16[27,16,16]{0,2,1:T(8,128)(2,1)} %param.6) | copy-start | bytes 41476
  8.1 36.7 %collective-permute-start = (bf16[12,480,128]{2,1,0:T(8,128)(2,1)}, bf16[12,480,128]{2,1,0:T(8,128)(2,1)}, u32[]{:S(2)}, u32[]{:S(2)}) collective-permute-start(bf16[12,480,128]{2,1,0:T(8,128)(2,1)} %get-tuple-element.18), channel_id=1, source_target_pairs={{0,1},{1,0},{2,3},{3,2},{4,5},{5,4},{6,7},{7,6},{8,9},{9,8},{10,11... | collective-permute-start | bytes 4423688 | tf_op jit(solution)/shard_map/ppermute | solution.py:446
  8.6 21.8 %collective-permute-start.5 = (bf16[4,80,128]{2,1,0:T(8,128)(2,1)}, bf16[4,80,128]{2,1,0:T(8,128)(2,1)S(1)}, u32[]{:S(2)}, u32[]{:S(2)}) collective-permute-start(bf16[4,80,128]{2,1,0:T(8,128)(2,1)} %get-tuple-element.23), channel_id=1, source_target_pairs={{0,6},{2,4},{4,10},{5,3},{6,8},{7,1},{8,14},{9,7},{10,12},{11,5},{... | collective-permute-start | bytes 245768 | tf_op jit(solution)/shard_map/ppermute | solution.py:446
  14.0 16.9 %collective-permute-start.6 = (bf16[4,80,128]{2,1,0:T(8,128)(2,1)}, bf16[4,80,128]{2,1,0:T(8,128)(2,1)}, u32[]{:S(2)}, u32[]{:S(2)}) collective-permute-start(bf16[4,80,128]{2,1,0:T(8,128)(2,1)} %get-tuple-element.24), channel_id=1, source_target_pairs={{1,6},{3,4},{4,3},{5,10},{6,1},{7,8},{8,7},{9,14},{10,5},{11,12},{... | collective-permute-start | bytes 245768 | tf_op jit(solution)/shard_map/ppermute | solution.py:446
  15.2 29.5 %collective-permute-start.1 = (bf16[4,480,128]{2,1,0:T(8,128)(2,1)}, bf16[4,480,128]{2,1,0:T(8,128)(2,1)}, u32[]{:S(2)}, u32[]{:S(2)}) collective-permute-start(bf16[4,480,128]{2,1,0:T(8,128)(2,1)} %get-tuple-element.19), channel_id=1, source_target_pairs={{0,4},{2,6},{4,8},{5,1},{6,10},{7,3},{8,12},{9,5},{10,14},{11,7},{... | collective-permute-start | bytes 1474568 | tf_op jit(solution)/shard_map/ppermute | solution.py:446
  20.2 24.6 %collective-permute-start.2 = (bf16[4,480,128]{2,1,0:T(8,128)(2,1)}, bf16[4,480,128]{2,1,0:T(8,128)(2,1)}, u32[]{:S(2)}, u32[]{:S(2)}) collective-permute-start(bf16[4,480,128]{2,1,0:T(8,128)(2,1)} %get-tuple-element.20), channel_id=1, source_target_pairs={{1,4},{3,6},{4,1},{5,8},{6,3},{7,10},{8,5},{9,12},{10,7},{11,14},{... | collective-permute-start | bytes 1474568 | tf_op jit(solution)/shard_map/ppermute | solution.py:446
  25.8 1.0 copy-start.4
  30.4 3.6 %copy-start.2 = (bf16[4,80,128]{2,1,0:T(8,128)(2,1)}, bf16[4,80,128]{2,1,0:T(8,128)(2,1)S(1)}, u32[]{:S(2)}) copy-start(bf16[4,80,128]{2,1,0:T(8,128)(2,1)S(1)} %collective-permute-done.5.refs_7_.refs_11_) | copy-start | bytes 245764
  30.4 9.3 %collective-permute-start.3 = (bf16[12,80,128]{2,1,0:T(8,128)(2,1)}, bf16[12,80,128]{2,1,0:T(8,128)(2,1)}, u32[]{:S(2)}, u32[]{:S(2)}) collective-permute-start(bf16[12,80,128]{2,1,0:T(8,128)(2,1)} %get-tuple-element.21), channel_id=1, source_target_pairs={{0,2},{1,3},{2,0},{3,1},{4,6},{5,7},{6,4},{7,5},{8,10},{9,11},{10,... | collective-permute-start | bytes 737288 | tf_op jit(solution)/shard_map/ppermute | solution.py:446
  30.9 13.9 %collective-permute-start.4 = (bf16[12,80,128]{2,1,0:T(8,128)(2,1)}, bf16[12,80,128]{2,1,0:T(8,128)(2,1)}, u32[]{:S(2)}, u32[]{:S(2)}) collective-permute-start(bf16[12,80,128]{2,1,0:T(8,128)(2,1)} %get-tuple-element.22), channel_id=1, source_target_pairs={{0,3},{1,2},{2,1},{3,0},{4,7},{5,6},{6,5},{7,4},{8,11},{9,10},{10,... | collective-permute-start | bytes 737288 | tf_op jit(solution)/shard_map/ppermute | solution.py:446
  34.0 2.0 %copy-start = (bf16[3,1,16,480]{2,3,0,1:T(8,128)(2,1)S(1)}, bf16[3,1,16,480]{2,3,0,1:T(8,128)(2,1)}, u32[]{:S(2)}) copy-start(bf16[3,1,16,480]{2,3,0,1:T(8,128)(2,1)} %get-tuple-element.46) | copy-start | bytes 138244
  35.4 9.4 %copy-start.5 = (f32[16]{0:T(128)S(1)}, f32[16]{0:T(128)}, u32[]{:S(2)}) copy-start(f32[16]{0:T(128)} %param.7) | copy-start | bytes 196
  93.4 17.5 %copy-start.1 = (bf16[16,8,24,128]{3,2,1,0:T(8,128)(2,1)S(1)}, bf16[16,8,24,128]{3,2,1,0:T(8,128)(2,1)}, u32[]{:S(2)}) copy-start(bf16[16,8,24,128]{3,2,1,0:T(8,128)(2,1)} %get-tuple-element.28) | copy-start | bytes 2359300
  93.4 17.5 %collective-permute-start.12 = (bf16[16,8,24,128]{3,2,1,0:T(8,128)(2,1)}, bf16[16,8,24,128]{3,2,1,0:T(8,128)(2,1)S(1)}, u32[]{:S(2)}, u32[]{:S(2)}) collective-permute-start(bf16[16,8,24,128]{3,2,1,0:T(8,128)(2,1)} %get-tuple-element.29), channel_id=1, source_target_pairs={{0,1},{1,0},{2,3},{3,2},{4,5},{5,4},{6,7},{7,6},{8,9},{9,8},{10,11... | collective-permute-start | bytes 2359304 | tf_op jit(solution)/shard_map/ppermute | solution.py:446
  93.5 12.2 %collective-permute-start.7 = (f32[8,24,128]{2,1,0:T(8,128)}, f32[8,24,128]{2,1,0:T(8,128)S(1)}, u32[]{:S(2)}, u32[]{:S(2)}) collective-permute-start(f32[8,24,128]{2,1,0:T(8,128)} %get-tuple-element.26), channel_id=1, source_target_pairs={{0,1},{1,0},{2,3},{3,2},{4,5},{5,4},{6,7},{7,6},{8,9},{9,8},{10,11... | collective-permute-start | bytes 294920 | tf_op jit(solution)/shard_map/ppermute | solution.py:446
  94.0 2.2 %collective-permute-start.8 = (f32[56,128]{1,0:T(8,128)}, f32[56,128]{1,0:T(8,128)S(1)}, u32[]{:S(2)}, u32[]{:S(2)}) collective-permute-start(f32[56,128]{1,0:T(8,128)} %get-tuple-element.27), channel_id=1, source_target_pairs={{0,1},{1,0},{2,3},{3,2},{4,5},{5,4},{6,7},{7,6},{8,9},{9,8},{10,11... | collective-permute-start | bytes 86024 | tf_op jit(solution)/shard_map/ppermute | solution.py:446
  96.9 3.9 %collective-permute-start.9 = (f32[56,128]{1,0:T(8,128)S(1)}, f32[56,128]{1,0:T(8,128)S(1)}, u32[]{:S(2)}, u32[]{:S(2)}) collective-permute-start(f32[56,128]{1,0:T(8,128)S(1)} %add.44), channel_id=1, source_target_pairs={{0,2},{2,0},{1,3},{3,1},{4,6},{6,4},{5,7},{7,5},{8,10},{10,8},{9,1... | collective-permute-start | bytes 86024 | tf_op jit(solution)/shard_map/ppermute | solution.py:501
  100.8 3.9 %collective-permute-start.10 = (f32[56,128]{1,0:T(8,128)S(1)}, f32[56,128]{1,0:T(8,128)S(1)}, u32[]{:S(2)}, u32[]{:S(2)}) collective-permute-start(f32[56,128]{1,0:T(8,128)S(1)} %add.45), channel_id=1, source_target_pairs={{0,4},{4,0},{8,12},{12,8},{1,5},{5,1},{9,13},{13,9},{2,6},{6,2},{1... | collective-permute-start | bytes 86024 | tf_op jit(solution)/shard_map/ppermute | solution.py:501
  104.6 4.8 %collective-permute-start.11 = (f32[56,128]{1,0:T(8,128)S(1)}, f32[56,128]{1,0:T(8,128)S(1)}, u32[]{:S(2)}, u32[]{:S(2)}) collective-permute-start(f32[56,128]{1,0:T(8,128)S(1)} %add.46), channel_id=1, source_target_pairs={{0,8},{4,12},{8,0},{12,4},{1,9},{5,13},{9,1},{13,5},{2,10},{6,14},... | collective-permute-start | bytes 86024 | tf_op jit(solution)/shard_map/ppermute | solution.py:501
where the time goes:
time: 113 us; the launch traced here: 112 us
  Pallas kernels  54.7 us (48%)
  starting transfers between devices  19.3 us (17%)
  local copies, waits for them, and re-layouts  17.9 us (16%)
  waiting for transfers between devices  15.6 us (14%)
  other arithmetic  3.73 us (3%)
    pallas_call x1, Pallas kernels, main(): pl.pallas_call(lambda *refs: main_kernel(channels, rows, *refs), out_shap...  47.9 us
    ppermute x10, starting transfers between devices, send(): return lax.ppermute(value, GROUP, routes(sizes, target))  16.9 us
    ppermute x3, waiting for transfers between devices, local(): lax.ppermute(grads, axis, [(i, i ^ step) for i in range(count)])  8.4 us
    ppermute x10, waiting for transfers between devices, send(): return lax.ppermute(value, GROUP, routes(sizes, target))  7.2 us
    pallas_call x1, Pallas kernels, pack(): pl.pallas_call(lambda *refs: pack_kernel(sides, *refs), out_shape=[jax.Sh...  6.79 us
    another operation x10, local copies, waits for them, and re-layouts, banded_weights(): forward = jnp.stack([band(base, y) for y in range(8)], axis=1)  5.66 us
    unnamed x21, local copies, waits for them, and re-layouts  5.44 us
    another operation x10, local copies, waits for them, and re-layouts, banded_weights(): backward = jnp.stack([band(flipped, y) for y in range(8)], axis=2)  4.72 us
  transfers between devices with their start and end apart: 13, of which 5 were waited for; matrix products, arithmetic and copies ran while one was open for 17% of the time, Pallas kernels for 0%

commit v1 on v0

v1 whole, which is shorter than its diff:
```python
import jax
import jax.numpy as jnp
from jax import lax
from jax.experimental import pallas as pl
from jax.experimental.pallas import tpu as pltpu
from jax.sharding import PartitionSpec as P

GROUP = ("gx", "gy", "gz")
HALO = 4
F32 = jnp.float32
BF16 = jnp.bfloat16


def routes(sizes, target):
    nx, ny, nz = sizes
    pairs = []
    for x in range(nx):
        for y in range(ny):
            for z in range(nz):
                tx, ty, tz = target(x, y, z)
                if 0 <= tx < nx and 0 <= ty < ny:
                    pairs.append(((x * ny + y) * nz + z, (tx * ny + ty) * nz + tz))
    return pairs


def pack_kernel(sides, feats, perm, source, own, swap, near, far, *edges):
    half = lax.axis_index("gz")
    at_y = lax.axis_index("gy")
    channels, planes, rows, lanes = feats.shape
    count = channels * rows
    row_id = lax.broadcasted_iota(jnp.int32, (count, count), 0)
    col_id = lax.broadcasted_iota(jnp.int32, (count, count), 1)
    order = (row_id % channels) * rows + row_id // channels
    permute = jnp.where(order == col_id, 1.0, 0.0).astype(BF16)
    wide = planes - HALO

    def put(ref, index, limit, value):
        @pl.when((index >= 0) & (index < limit))
        def _():
            ref[index] = value

    def pair_step(pair, carry):
        x0 = pair * 2
        parts = [feats[:, x0 + j].astype(F32).reshape(count, lanes).astype(BF16) for j in range(2)]
        moved = jnp.dot(permute, jnp.concatenate(parts, axis=1), preferred_element_type=F32)
        for j in range(2):
            x = x0 + j
            cells = moved[:, j * lanes : (j + 1) * lanes]
            coefficient = perm[x]
            term = source[x]
            coefficient_hi = coefficient.astype(BF16).astype(F32)
            term_hi = term.astype(BF16).astype(F32)
            extra = [coefficient_hi, coefficient - coefficient_hi, term_hi, term - term_hi]
            plane = jnp.concatenate([cells] + extra, axis=0).astype(BF16)
            own[x] = plane
            put(swap, x - HALO * (1 - half), wide, plane)
            high = x - wide
            put(near, jnp.where(half == 0, high, x), HALO, plane)
            put(far, jnp.where(half == 0, x, high), HALO, plane)
            pieces = []
            for start in (rows - HALO, 0):
                lines = [cells[start * channels : (start + HALO) * channels]]
                pieces.append(jnp.concatenate(lines + [e[start : start + HALO] for e in extra], axis=0))
            if sides == 1:
                pieces = [jnp.where(at_y == 0, pieces[0], pieces[1])]
            for side in range(sides):
                edges[side][x] = pieces[side].astype(BF16)
        return carry

    lax.fori_loop(0, planes // 2, pair_step, 0)


def pack(feats, perm, source, sides):
    channels, planes, rows, lanes = feats.shape
    full = rows * (channels + 4)
    edge = HALO * (channels + 4)
    shapes = [(planes, full), (planes - HALO, full), (HALO, full), (HALO, full)] + [(planes, edge)] * sides
    vmem = pl.BlockSpec(memory_space=pltpu.VMEM)
    return pl.pallas_call(
        lambda *refs: pack_kernel(sides, *refs),
        out_shape=[jax.ShapeDtypeStruct(s + (lanes,), BF16) for s in shapes],
        in_specs=[vmem] * 3,
        out_specs=[vmem] * len(shapes),
        name="pack",
    )(feats, perm, source)


def weights_kernel(base, forward, backward):
    channels = base.shape[2]
    taps = 3 * channels
    block = 8 * channels
    width = forward.shape[1]
    size = -(-width // 128) * 128
    blank = jnp.zeros((channels, size - 3 * taps), F32)
    place = lax.broadcasted_iota(jnp.int32, (block, size), 0) % 8
    for dx in range(3):
        line = jnp.concatenate([base[0, dx].astype(F32), blank], axis=1)
        for y in range(8):
            moved = line if y == 0 else pltpu.roll(line, y * taps, 1)
            start = dx * block + y * channels
            forward[start : start + channels, :] = moved[:, :width].astype(BF16)
        line = jnp.concatenate([base[1, dx].astype(F32), blank], axis=1)
        lines = jnp.broadcast_to(line[:, None, :], (channels, 8, size)).reshape(block, size)
        out = lines
        for y in range(1, 8):
            out = jnp.where(place == y, pltpu.roll(lines, y * taps, 1), out)
        backward[dx * block : (dx + 1) * block, :] = out[:, :width].astype(BF16)


def banded_weights(kernel):
    channels = kernel.shape[1]
    grid = kernel.reshape(3, 9, channels, channels)
    base = grid.transpose(0, 2, 1, 3).reshape(3, channels, 9 * channels)
    flipped = grid[::-1, ::-1].transpose(0, 3, 1, 2).reshape(3, channels, 9 * channels)
    vmem = pl.BlockSpec(memory_space=pltpu.VMEM)
    shape = jax.ShapeDtypeStruct((24 * channels, 30 * channels), BF16)
    return pl.pallas_call(
        weights_kernel, out_shape=[shape, shape], in_specs=[vmem], out_specs=[vmem, vmem], name="weights"
    )(jnp.stack([base, flipped]))


def sigmoid(value):
    return 0.5 * jnp.tanh(0.5 * value) + 0.5


def main_kernel(channels, rows, sides, proj, weights_fwd, weights_bwd, own, swap, near, far, *rest):
    edges = rest[: 4 * sides]
    (
        res_own, res_send, fg_own, fg_send, grads,
        raw_mine, raw_other, edge_mine, edge_other, sems,
        fwide, slot_a, slot_b, pre_ref, coef, src, vfield, face_x, face_y, face_z, rfield, afield,
        acc_a, acc_b, kacc, pacc,
    ) = rest[4 * sides :]
    half = lax.axis_index("gz")
    at_x = lax.axis_index("gx")
    at_y = lax.axis_index("gy")
    has_xlo = (at_x > 0) | (half == 1)
    has_xhi = (at_x < lax.axis_size("gx") - 1) | (half == 0)
    has_ylo = at_y > 0
    has_yhi = at_y < lax.axis_size("gy") - 1
    lanes = own.shape[2]
    zsize = 2 * lanes
    ext_y = rows + 2 * HALO
    wide = swap.shape[0]
    ext_x = wide + HALO
    inner = ext_x - 2 * HALO
    taps = 3 * channels
    window = 10 * taps
    block = 8 * channels
    yblocks = ext_y // 8
    oblocks = rows // 8
    cell_rows = rows * channels
    edge_rows = HALO * channels

    most = pl.ds(HALO * (1 - half), wide)
    side_part = pl.ds(wide * half, HALO)
    held = pl.ds(HALO * half, wide)
    moves = [
        (own.at[held], raw_mine.at[most]),
        (near, raw_mine.at[side_part]),
        (swap, raw_other.at[most]),
        (far, raw_other.at[side_part]),
    ]
    for s in range(sides):
        e_own, e_swap, e_near, e_far = edges[4 * s : 4 * s + 4]
        moves += [
            (e_own.at[held], edge_mine.at[s, most]),
            (e_near, edge_mine.at[s, side_part]),
            (e_swap.at[held], edge_other.at[s, most]),
            (e_far, edge_other.at[s, side_part]),
        ]
    copies = [pltpu.make_async_copy(a, b, sems.at[k]) for k, (a, b) in enumerate(moves)]
    for copy in copies:
        copy.start()

    lane_row = lax.broadcasted_iota(jnp.int32, (1, zsize), 1)
    not_first = jnp.where(lane_row == 0, 0.0, 1.0).astype(BF16)
    not_last = jnp.where(lane_row == zsize - 1, 0.0, 1.0).astype(BF16)
    sub = lax.broadcasted_iota(jnp.int32, (channels, zsize), 0)
    proj_rows = jnp.zeros((channels, zsize), F32)
    tile_lane = lax.broadcasted_iota(jnp.int32, (16, 2 * block), 1) % block
    tile_row = lax.broadcasted_iota(jnp.int32, (16, 2 * block), 0)
    tile_low = lax.broadcasted_iota(jnp.int32, (16, 2 * block), 1) < block
    proj_lanes = jnp.zeros((16, 2 * block), F32)
    for c in range(channels):
        proj_rows = jnp.where(sub == c, proj[c], proj_rows)
        proj_lanes = jnp.where(tile_lane % channels == c, proj[c], proj_lanes)
    proj_block = jnp.concatenate([proj_rows] * 8, axis=0)
    proj_hi = proj_lanes.astype(BF16).astype(F32)
    on_row = tile_lane // channels == tile_row % 8
    reduce_hi = jnp.where(on_row & (tile_row < 8), proj_hi, 0.0)
    reduce_lo = jnp.where(on_row & (tile_row >= 8) & tile_low, proj_lanes - proj_hi, 0.0)
    reducer = (reduce_hi + reduce_lo).astype(BF16)
    row_index = lax.broadcasted_iota(jnp.int32, (ext_y, zsize), 0)
    y_inside = ((row_index >= HALO) | has_ylo) & ((row_index < HALO + rows) | has_yhi)
    lane_index = lax.broadcasted_iota(jnp.int32, (ext_y, zsize), 1)
    zero = jnp.zeros((1, taps, lanes), BF16)
    for e in range(ext_x):
        for s in range(2):
            fwide[e, s, 0:1] = zero
            fwide[e, s, ext_y + 1 : ext_y + 2] = zero
    kacc[...] = jnp.zeros(kacc.shape, F32)
    pacc[...] = jnp.zeros(pacc.shape, F32)
    acc_a[...] = jnp.zeros(acc_a.shape, F32)
    acc_b[...] = jnp.zeros(acc_b.shape, F32)
    for copy in copies:
        copy.wait()

    def spread(ref, value, y0):
        n = value.shape[0] // channels
        below = pltpu.roll(value, 1, 1) * not_first
        above = pltpu.roll(value, zsize - 1, 1) * not_last
        for tap, shifted in enumerate((below, value, above)):
            for s in range(2):
                piece = shifted[:, s * lanes : (s + 1) * lanes].reshape(n, channels, lanes)
                ref[s, y0 : y0 + n, tap * channels : (tap + 1) * channels, :] = piece

    def joined(mine, other):
        return jnp.concatenate([jnp.where(half == 0, mine, other), jnp.where(half == 0, other, mine)], axis=1)

    def part(e, start, stop):
        return joined(raw_mine[e, start:stop], raw_other[e, start:stop])

    def edge_part(s, e, start, stop):
        return joined(edge_mine[s, e, start:stop], edge_other[s, e, start:stop])

    def face(a, b):
        return 2.0 * a * b / (a + b)

    def fill_cells(e, k):
        start = 8 * k - HALO
        lo = max(start, 0)
        hi = min(start + 8, rows)
        value = part(e, lo * channels, hi * channels)
        blank = jnp.zeros((edge_rows, zsize), BF16)
        if start < 0:
            value = jnp.concatenate([jnp.where(has_ylo, edge_part(0, e, 0, edge_rows), blank), value], axis=0)
        if start + 8 > rows:
            value = jnp.concatenate([value, jnp.where(has_yhi, edge_part(sides - 1, e, 0, edge_rows), blank)], axis=0)
        spread(fwide.at[e], value, 8 * k + 1)

    def fill_fields(e):
        centre = part(e, cell_rows, cell_rows + 4 * rows).astype(F32)
        low = edge_part(0, e, edge_rows, edge_rows + 4 * HALO).astype(F32)
        high = edge_part(sides - 1, e, edge_rows, edge_rows + 4 * HALO).astype(F32)

        def full(kind):
            def at(value, n):
                start = kind * n
                return value[start : start + n] + value[start + n : start + 2 * n]

            mid = at(centre, rows)
            first = jnp.where(has_ylo, at(low, HALO), mid[0:1])
            last = jnp.where(has_yhi, at(high, HALO), mid[rows - 1 : rows])
            return jnp.concatenate([first, mid, last], axis=0)

        plane = full(0)
        coef[e] = plane
        src[e] = full(2)
        face_y[e] = face(plane, pltpu.roll(plane, ext_y - 1, 0))
        face_z[e] = jnp.where(lane_index == zsize - 1, plane, face(plane, pltpu.roll(plane, zsize - 1, 1)))
        before = jnp.maximum(e - 1, 0)
        face_x[before] = face(coef[before], plane)

    def x_inside(e):
        return ((e >= HALO) | has_xlo) & ((e < ext_x - HALO) | has_xhi)

    def masked(e, value):
        return jnp.where(y_inside & x_inside(e), value, 0.0)

    def taps_of(ref, y0):
        return jnp.concatenate([ref[s, y0 : y0 + 10].reshape(window, lanes) for s in range(2)], axis=1)

    def convolve(e, yb):
        result = jnp.dot(weights_fwd[...], taps_of(fwide.at[e], 8 * yb), preferred_element_type=F32)
        pre_ref[jnp.maximum(e - 2, 0), yb] = acc_b[yb] + result[2 * block :]
        acc_b[yb] = acc_a[yb] + result[block : 2 * block]
        acc_a[yb] = result[:block]

    def activate(px, yb):
        pre = pre_ref[px, yb]
        active = pre * sigmoid(pre)
        high = active.astype(BF16)
        low = (active - high.astype(F32)).astype(BF16)
        sums = jnp.dot(reducer, jnp.concatenate([high, low], axis=0), preferred_element_type=F32)
        inside = y_inside[8 * yb : 8 * yb + 8] & x_inside(px + 1)
        vfield[px, 8 * yb : 8 * yb + 8, :] = jnp.where(inside, sums[:8] + sums[8:], 0.0)

    for k in range(yblocks):
        fill_cells(0, k)
    fill_fields(0)

    def conv_step(e, carry):
        for k in range(yblocks):
            activate(jnp.maximum(e - 4, 0), k)
            convolve(e - 1, k)
            fill_cells(e, k)
        fill_fields(e)
        return carry

    lax.fori_loop(1, ext_x, conv_step, 0)
    for k in range(yblocks):
        activate(ext_x - 4, k)
        convolve(ext_x - 1, k)
    for k in range(yblocks):
        activate(ext_x - 3, k)

    @pl.when(jnp.logical_not(has_xlo))
    def _():
        face_x[HALO - 1] = coef[HALO]

    @pl.when(jnp.logical_not(has_xhi))
    def _():
        face_x[ext_x - HALO - 1] = coef[ext_x - HALO - 1]

    def operator(e, below, centre, above):
        flux_y = face_y[e] * (centre - pltpu.roll(centre, ext_y - 1, 0))
        next_z = jnp.where(lane_index == zsize - 1, 0.0, pltpu.roll(centre, zsize - 1, 1))
        flux_z = face_z[e] * (centre - next_z)
        left_z = jnp.where(lane_index == 0, -coef[e] * centre, pltpu.roll(flux_z, 1, 1))
        total = face_x[e] * (centre - above) + face_x[e - 1] * (centre - below)
        return total + (flux_y - pltpu.roll(flux_y, 1, 0)) + (flux_z - left_z)

    def residual_step(i, carry):
        value = operator(i + 2, vfield[i], vfield[i + 1], vfield[i + 2]) - src[i + 2]
        rfield[i] = masked(i + 2, value)
        return carry

    lax.fori_loop(0, ext_x - 4, residual_step, 0, unroll=4)

    def adjoint_step(i, carry):
        afield[i] = masked(i + 3, operator(i + 3, rfield[i], rfield[i + 1], rfield[i + 2]))
        return carry

    lax.fori_loop(0, ext_x - 6, adjoint_step, 0, unroll=5)

    def residual_out(x, carry):
        value = rfield[x + 2][HALO : HALO + rows]
        low = value[:, :lanes]
        high = value[:, lanes:]
        res_own[x] = jnp.where(half == 0, low, high)
        res_send[x] = jnp.where(half == 0, high, low)
        return carry

    lax.fori_loop(0, inner, residual_out, 0, unroll=4)

    def grad_block(i, yb, slot):
        pre = pre_ref[i + 2, yb]
        sig = sigmoid(pre)
        near_adj = afield[i, 8 * yb : 8 * yb + 8, :]
        adj = jnp.broadcast_to(near_adj[:, None, :], (8, channels, zsize)).reshape(block, zsize)
        slope = sig * (1.0 + pre * (1.0 - sig))
        spread(slot, (adj * proj_block * slope).astype(BF16), 8 * yb + 1)
        lo = max(HALO - 8 * yb, 0)
        hi = min(HALO + rows - 8 * yb, 8)
        term = (adj * (pre * sig))[lo * channels : hi * channels]
        total = term[:channels]
        for y in range(1, hi - lo):
            total = total + term[y * channels : (y + 1) * channels]
        pacc[...] += jnp.where((i >= 1) & (i <= inner), total, 0.0)

    def back_product(b, slot, weights):
        return jnp.dot(weights, taps_of(slot, HALO + 8 * b), preferred_element_type=F32)

    def store_plane(x, parts):
        value = jnp.concatenate([p.reshape(channels, 8, zsize) for p in parts], axis=1).astype(BF16)
        low = value[:, :, :lanes]
        high = value[:, :, lanes:]
        fg_own[:, x] = jnp.where(half == 0, low, high)
        fg_send[:, x] = jnp.where(half == 0, high, low)

    def multiply(i, slot, make):
        parts = []
        centres = []
        for b in range(oblocks):
            y0 = HALO + 1 + 8 * b
            pieces = [slot[s, y0 : y0 + 8, channels : 2 * channels, :].reshape(block, lanes) for s in range(2)]
            centres.append(jnp.concatenate(pieces, axis=1))
        for k in range(max(3, oblocks, yblocks)):
            if k < oblocks:
                result = back_product(k, slot, weights_bwd[...])
                parts.append(acc_b[k] + result[2 * block :])
                acc_b[k] = acc_a[k] + result[block : 2 * block]
                acc_a[k] = result[:block]
            if k < 3:
                total = kacc[k]
                for b in range(oblocks):
                    total = total + lax.dot_general(
                        taps_of(fwide.at[i + HALO - 2 + k], HALO + 8 * b),
                        centres[b],
                        (((1,), (1,)), ((), ())),
                        preferred_element_type=F32,
                    )
                kacc[k] = total
            if k < yblocks:
                make(k)
        store_plane(jnp.maximum(i - 2, 0), parts)

    for k in range(yblocks):
        grad_block(0, k, slot_a)
    for b in range(oblocks):
        acc_a[b] = back_product(b, slot_a, weights_bwd[:block])
        acc_b[b] = jnp.zeros((block, zsize), F32)
    for k in range(yblocks):
        grad_block(1, k, slot_b)

    def grad_step(t, carry):
        odd = 2 * t - 1
        multiply(odd, slot_b, lambda k: grad_block(odd + 1, k, slot_a))
        multiply(odd + 1, slot_a, lambda k: grad_block(odd + 2, k, slot_b))
        return carry

    lax.fori_loop(1, inner // 2 + 1, grad_step, 0)
    store_plane(inner - 1, [acc_b[b] + back_product(b, slot_b, weights_bwd[2 * block :]) for b in range(oblocks)])

    lane_group = lax.broadcasted_iota(jnp.int32, (3 * taps, block), 1) // channels
    sub_row = lax.broadcasted_iota(jnp.int32, (3 * taps, block), 0) % (block // channels)
    per_dx = 3 * taps * channels // block
    for dx in range(3):
        picked = jnp.zeros((3 * taps, block), F32)
        for y in range(8):
            picked = jnp.where(lane_group == y, kacc[dx, y * taps : y * taps + 3 * taps], picked)
        step = channels
        while step < block:
            picked = picked + pltpu.roll(picked, step, 1)
            step *= 2
        packed = jnp.where(lane_group == sub_row, picked, 0.0).reshape(per_dx, block // channels, block)
        grads[dx * per_dx : (dx + 1) * per_dx, :] = jnp.sum(packed, axis=1)
    per_channel = jnp.sum(pacc[...], axis=1, keepdims=True)
    chan_row = lax.broadcasted_iota(jnp.int32, (channels, block), 0)
    chan_lane = lax.broadcasted_iota(jnp.int32, (channels, block), 1)
    flat = jnp.sum(jnp.where(chan_row == chan_lane, per_channel, 0.0), axis=0, keepdims=True)
    grads[3 * per_dx :, :] = jnp.broadcast_to(flat, (grads.shape[0] - 3 * per_dx, block))


def main(channels, rows, proj, weights, tensors, edges):
    own, swap = tensors[0], tensors[1]
    sides = len(edges) // 4
    lanes = own.shape[2]
    zsize = 2 * lanes
    wide = swap.shape[0]
    ext_x = wide + HALO
    ext_y = rows + 2 * HALO
    inner = ext_x - 2 * HALO
    taps = 3 * channels
    block = 8 * channels
    yblocks = ext_y // 8
    grad_rows = 27 * channels * channels // block
    out_rows = -(-(grad_rows + 1) // 8) * 8
    vmem = pl.BlockSpec(memory_space=pltpu.VMEM)
    anywhere = pl.BlockSpec(memory_space=pl.ANY)
    plane = (ext_y, zsize)
    slot = pltpu.VMEM((2, ext_y + 2, taps, lanes), BF16)
    return pl.pallas_call(
        lambda *refs: main_kernel(channels, rows, sides, *refs),
        out_shape=[
            jax.ShapeDtypeStruct((inner, rows, lanes), F32),
            jax.ShapeDtypeStruct((inner, rows, lanes), F32),
            jax.ShapeDtypeStruct((channels, inner, rows, lanes), BF16),
            jax.ShapeDtypeStruct((channels, inner, rows, lanes), BF16),
            jax.ShapeDtypeStruct((out_rows, block), F32),
        ],
        in_specs=[pl.BlockSpec(memory_space=pltpu.SMEM)] + [vmem] * 2 + [anywhere] * (len(tensors) + len(edges)),
        out_specs=[vmem] * 5,
        scratch_shapes=[
            pltpu.VMEM((ext_x,) + own.shape[1:], BF16),
            pltpu.VMEM((ext_x,) + own.shape[1:], BF16),
            pltpu.VMEM((sides, ext_x) + edges[0].shape[1:], BF16),
            pltpu.VMEM((sides, ext_x) + edges[0].shape[1:], BF16),
            pltpu.SemaphoreType.DMA((4 + 4 * sides,)),
            pltpu.VMEM((ext_x, 2, ext_y + 2, taps, lanes), BF16),
            slot,
            slot,
            pltpu.VMEM((ext_x - 2, yblocks, block, zsize), F32),
            pltpu.VMEM((ext_x,) + plane, F32),
            pltpu.VMEM((ext_x,) + plane, F32),
            pltpu.VMEM((ext_x - 2,) + plane, F32),
            pltpu.VMEM((ext_x,) + plane, F32),
            pltpu.VMEM((ext_x,) + plane, F32),
            pltpu.VMEM((ext_x,) + plane, F32),
            pltpu.VMEM((ext_x - 4,) + plane, F32),
            pltpu.VMEM((ext_x - 6,) + plane, F32),
            pltpu.VMEM((yblocks, block, zsize), F32),
            pltpu.VMEM((yblocks, block, zsize), F32),
            pltpu.VMEM((3, 10 * taps, block), F32),
            pltpu.VMEM((channels, zsize), F32),
        ],
        compiler_params=pltpu.CompilerParams(vmem_limit_bytes=58 * 1024 * 1024),
        name="step",
    )(proj, *weights, *tensors, *edges)


def local(feats, kernel, proj, perm, source):
    channels, planes, rows, lanes = feats.shape
    sizes = tuple(lax.axis_size(a) for a in GROUP)
    ny = sizes[1]
    half = lax.axis_index("gz")
    sides = 1 if ny == 2 else 2

    def send(value, target):
        return lax.ppermute(value, GROUP, routes(sizes, target))

    def partner(value):
        return send(value, lambda x, y, z: (x, y, 1 - z))

    def to_near(value):
        return send(value, lambda x, y, z: (x + 1 if z == 0 else x - 1, y, z))

    def to_far(value):
        return send(value, lambda x, y, z: (x - 1 if z == 0 else x + 1, y, 1 - z))

    own, swap, near, far, *edges = pack(feats, perm, source, sides)
    received = []
    for side in range(sides):

        def step_y(y, side=side):
            if sides == 1:
                return 1 - y
            return y + 1 if side == 0 else y - 1

        received.append(send(edges[side], lambda x, y, z: (x, step_y(y), z)))
    tensors = [own, partner(swap), to_near(near), to_far(far)]
    wide = planes - HALO
    got = []
    for value in received:
        got += [
            value,
            partner(value),
            to_near(lax.dynamic_slice_in_dim(value, wide * (1 - half), HALO, 0)),
            to_far(lax.dynamic_slice_in_dim(value, wide * half, HALO, 0)),
        ]
    weights = banded_weights(kernel)
    res_own, res_send, fg_own, fg_send, grads = main(channels, rows, proj, weights, tensors, got)

    res_got = partner(res_send)
    fg_got = partner(fg_send)

    def ordered(mine, other, axis):
        return jnp.where(
            half == 0, jnp.concatenate([mine, other], axis), jnp.concatenate([other, mine], axis)
        )

    residual = ordered(res_own, res_got, 0)
    feats_grad = ordered(fg_own, fg_got, 1)
    grads = grads + partner(grads)
    for axis in ("gy", "gx"):
        count = lax.axis_size(axis)
        step = 1
        while step < count:
            grads = grads + lax.ppermute(grads, axis, [(i, i ^ step) for i in range(count)])
            step *= 2
    grad_rows = 27 * channels * channels // grads.shape[1]
    kernel_grad = grads[:grad_rows].reshape(27, channels, channels).transpose(0, 2, 1)
    proj_grad = grads[grad_rows, :channels]
    return (residual, kernel_grad, proj_grad, feats_grad)


def solution(mesh):
    in_specs = (
        P(None, ("grp", "gx"), "gy", "gz"),
        P(),
        P(),
        P(("grp", "gx"), "gy", "gz"),
        P(("grp", "gx"), "gy", "gz"),
    )
    out_specs = (
        P(("grp", "gx"), "gy", "gz"),
        P("grp", None, None),
        P("grp"),
        P(None, ("grp", "gx"), "gy", "gz"),
    )
    return jax.shard_map(local, mesh=mesh, in_specs=in_specs, out_specs=out_specs, check_vma=False)
```

time: 113 us -> 96.1 us (0.85)
  local copies, waits for them, and re-layouts: 17.9 us -> 4.31 us
  Pallas kernels: 54.7 us -> 50.4 us
  starting transfers between devices: 19.3 us -> 23.2 us
  waiting for transfers between devices: 15.6 us -> 12.6 us
    another operation x21 -> x2, local copies, waits for them, and re-layouts: 11 us -> 0.21 us  [banded_weights(): jnp.stack([base, flipped])]
    pallas_call x1 -> x2, Pallas kernels: 47.9 us -> 44 us  [the longest x1 41.2 us: main(): pl.pallas_call(lambda *refs: main_kernel(channels, rows, sides, *refs), o...]
    unnamed x21 -> x18, local copies, waits for them, and re-layouts: 5.44 us -> 2.53 us
    ppermute x3, starting transfers between devices: 2.43 us -> 4.71 us  [local(): lax.ppermute(grads, axis, [(i, i ^ step) for i in range(count)])]
    ppermute x3, waiting for transfers between devices: 8.4 us -> 6.13 us  [local(): lax.ppermute(grads, axis, [(i, i ^ step) for i in range(count)])]
    ppermute x10, starting transfers between devices: 16.9 us -> 18.5 us  [send(): return lax.ppermute(value, GROUP, routes(sizes, target))]
  transfers between devices with their start and end apart: 13 -> 13, of which waited for: 5 -> 5; matrix products, arithmetic and copies ran while one was open for 17% -> 6% of each run, Pallas kernels for 0% -> 3%
where the time goes in v1:
time: 96.1 us; the launch traced here: 95.7 us
  Pallas kernels  50.4 us (52%)
  starting transfers between devices  23.2 us (24%)
  waiting for transfers between devices  12.6 us (13%)
  other arithmetic  4.35 us (5%)
  local copies, waits for them, and re-layouts  4.31 us (4%)
    pallas_call x1, Pallas kernels, main(): pl.pallas_call(lambda *refs: main_kernel(channels, rows, sides, *refs), o...  41.2 us
    ppermute x10, starting transfers between devices, send(): return lax.ppermute(value, GROUP, routes(sizes, target))  18.5 us
    ppermute x10, waiting for transfers between devices, send(): return lax.ppermute(value, GROUP, routes(sizes, target))  6.49 us
    pallas_call x1, Pallas kernels, pack(): pl.pallas_call(lambda *refs: pack_kernel(sides, *refs), out_shape=[jax.Sh...  6.4 us
    ppermute x3, waiting for transfers between devices, local(): lax.ppermute(grads, axis, [(i, i ^ step) for i in range(count)])  6.13 us
    ppermute x3, starting transfers between devices, local(): lax.ppermute(grads, axis, [(i, i ^ step) for i in range(count)])  4.71 us
    select_n x2, other arithmetic, ordered(): jnp.where(half == 0, jnp.concatenate([mine, other], axis), jnp.concatenat...  2.95 us
    pallas_call x1, Pallas kernels, banded_weights(): pl.pallas_call(weights_kernel, out_shape=[shape, shape], in_specs=[vmem],...  2.8 us
  transfers between devices with their start and end apart: 13, of which 5 were waited for; matrix products, arithmetic and copies ran while one was open for 6% of the time, Pallas kernels for 3%

profile of v1, /device:TPU:0, one launch (start us, length us, event | category | flops | bytes accessed | tf_op | source)
XLA Modules:
  0.0 95.7 jit_solution(4106699143035486278)
XLA Ops:
  0.6 6.4 %pack.1 = (bf16[16,480,128]{2,1,0:T(8,128)(2,1)}, bf16[12,480,128]{2,1,0:T(8,128)(2,1)}, bf16[4,480,128]{2,1,0:T(8,128)(2,1)}, bf16[4,480,128]{2,1,0:T(8,128)(2,1)}, bf16[16,80,128]{2,1,0:T(8,128)(2,1)}) custom-call(bf16[16,16,24,128]{3,2,1,0:T(8,128)(2,1)} %refs_0_.2, f32[16,24,128]{2,1,0:T(8,128)} %refs_1_.1, f32[16,24,128]{2,1,0:T(8,128)} %refs_2_.1), custom_call_target="tpu_custom_call" | custom-call | tf_op jit(solution)/shard_map/pack/pallas_call | solution.py:79
  7.0 0.5 collective-permute-start
  7.5 2.5 %collective-permute-start.3 = (bf16[16,80,128]{2,1,0:T(8,128)(2,1)}, bf16[16,80,128]{2,1,0:T(8,128)(2,1)S(1)}, u32[]{:S(2)}, u32[]{:S(2)}) collective-permute-start(bf16[16,80,128]{2,1,0:T(8,128)(2,1)} %get-tuple-element.22), channel_id=1, source_target_pairs={{0,2},{1,3},{2,0},{3,1},{4,6},{5,7},{6,4},{7,5},{8,10},{9,11},{10,... | collective-permute-start | bytes 983048 | tf_op jit(solution)/shard_map/ppermute | solution.py:501
  10.0 3.5 %collective-permute-start.1 = (bf16[4,480,128]{2,1,0:T(8,128)(2,1)}, bf16[4,480,128]{2,1,0:T(8,128)(2,1)S(1)}, u32[]{:S(2)}, u32[]{:S(2)}) collective-permute-start(bf16[4,480,128]{2,1,0:T(8,128)(2,1)} %get-tuple-element.20), channel_id=1, source_target_pairs={{0,4},{2,6},{4,8},{5,1},{6,10},{7,3},{8,12},{9,5},{10,14},{11,7},{... | collective-permute-start | bytes 1474568 | tf_op jit(solution)/shard_map/ppermute | solution.py:501
  13.5 0.7 collective-permute-start.2
  14.2 4.4 %collective-permute-done.3.refs_7_ = bf16[16,80,128]{2,1,0:T(8,128)(2,1)S(1)} collective-permute-done((bf16[16,80,128]{2,1,0:T(8,128)(2,1)}, bf16[16,80,128]{2,1,0:T(8,128)(2,1)S(1)}, u32[]{:S(2)}, u32[]{:S(2)}) %collective-permute-start.3) | collective-permute-done | bytes 327712 | tf_op jit(solution)/shard_map/ppermute | solution.py:501
  18.6 0.7 constant_dynamic-slice_fusion
  19.3 1.3 %collective-permute-start.6 = (bf16[4,80,128]{2,1,0:T(8,128)(2,1)}, bf16[4,80,128]{2,1,0:T(8,128)(2,1)}, u32[]{:S(2)}, u32[]{:S(2)}) collective-permute-start(bf16[4,80,128]{2,1,0:T(8,128)(2,1)} %get-tuple-element.32), channel_id=1, source_target_pairs={{1,4},{3,6},{4,1},{5,8},{6,3},{7,10},{8,5},{9,12},{10,7},{11,14},{... | collective-permute-start | bytes 245768 | tf_op jit(solution)/shard_map/ppermute | solution.py:501
  20.6 0.2 copy.17
  20.8 0.2 copy.12
  21.3 9.4 %collective-permute-start.5 = (bf16[4,80,128]{2,1,0:T(8,128)(2,1)S(1)}, bf16[4,80,128]{2,1,0:T(8,128)(2,1)S(1)}, u32[]{:S(2)}, u32[]{:S(2)}) collective-permute-start(bf16[4,80,128]{2,1,0:T(8,128)(2,1)S(1)} %get-tuple-element.33), channel_id=1, source_target_pairs={{0,4},{2,6},{4,8},{5,1},{6,10},{7,3},{8,12},{9,5},{10,14},{11,7},{... | collective-permute-start | bytes 245768 | tf_op jit(solution)/shard_map/ppermute | solution.py:501
  30.7 0.6 pad_maximum_fusion.base
  31.3 2.8 %weights.1 = (bf16[384,480]{1,0:T(8,128)(2,1)}, bf16[384,480]{1,0:T(8,128)(2,1)}) custom-call(bf16[2,3,16,144]{3,2,1,0:T(8,128)(2,1)} %pad_maximum_fusion.base), custom_call_target="tpu_custom_call" | custom-call | tf_op jit(solution)/shard_map/weights/pallas_call | solution.py:117
  34.2 0.5 copy-done.7
  34.7 0.2 copy-done.3
  34.9 0.2 copy-done.4
  35.2 0.5 copy-done
  35.7 41.2 %step.1 = (f32[8,24,128]{2,1,0:T(8,128)}, f32[8,24,128]{2,1,0:T(8,128)}, bf16[16,8,24,128]{3,2,1,0:T(8,128)(2,1)}, bf16[16,8,24,128]{3,2,1,0:T(8,128)(2,1)}, f32[56,128]{1,0:T(8,128)}) custom-call(f32[16]{0:T(128)} %refs_0_.3, bf16[384,480]{1,0:T(8,128)(2,1)} %get-tuple-element.16.refs_1_, bf16[384,480]{1,0:T(8,128)(2,1)} %get-tuple-element.17.refs_2_, ...), custom_call_target="tpu_custom_call" | custom-call | tf_op jit(solution)/shard_map/step/pallas_call | solution.py:454
  76.9 0.5 collective-permute-start.7
  77.5 2.1 %collective-permute-done.8 = f32[56,128]{1,0:T(8,128)S(1)} collective-permute-done((f32[56,128]{1,0:T(8,128)}, f32[56,128]{1,0:T(8,128)S(1)}, u32[]{:S(2)}, u32[]{:S(2)}) %collective-permute-start.8) | collective-permute-done | bytes 28704 | tf_op jit(solution)/shard_map/ppermute | solution.py:501
  79.6 0.8 add.20
  80.4 0.5 collective-permute-start.9
  80.9 3.3 %collective-permute-done.9 = f32[56,128]{1,0:T(8,128)S(1)} collective-permute-done((f32[56,128]{1,0:T(8,128)S(1)}, f32[56,128]{1,0:T(8,128)S(1)}, u32[]{:S(2)}, u32[]{:S(2)}) %collective-permute-start.9) | collective-permute-done | bytes 28704 | tf_op jit(solution)/shard_map/ppermute | solution.py:550
  84.2 1.6 %collective-permute-start.10 = (f32[56,128]{1,0:T(8,128)S(1)}, f32[56,128]{1,0:T(8,128)S(1)}, u32[]{:S(2)}, u32[]{:S(2)}) collective-permute-start(f32[56,128]{1,0:T(8,128)S(1)} %add.21), channel_id=1, source_target_pairs={{0,4},{4,0},{8,12},{12,8},{1,5},{5,1},{9,13},{13,9},{2,6},{6,2},{1... | collective-permute-start | bytes 86024 | tf_op jit(solution)/shard_map/ppermute | solution.py:550
  85.8 2.3 %collective-permute-done.10 = f32[56,128]{1,0:T(8,128)S(1)} collective-permute-done((f32[56,128]{1,0:T(8,128)S(1)}, f32[56,128]{1,0:T(8,128)S(1)}, u32[]{:S(2)}, u32[]{:S(2)}) %collective-permute-start.10) | collective-permute-done | bytes 28704 | tf_op jit(solution)/shard_map/ppermute | solution.py:550
  88.1 2.6 %collective-permute-start.11 = (f32[56,128]{1,0:T(8,128)S(1)}, f32[56,128]{1,0:T(8,128)S(1)}, u32[]{:S(2)}, u32[]{:S(2)}) collective-permute-start(f32[56,128]{1,0:T(8,128)S(1)} %add.22), channel_id=1, source_target_pairs={{0,8},{4,12},{8,0},{12,4},{1,9},{5,13},{9,1},{13,5},{2,10},{6,14},... | collective-permute-start | bytes 86024 | tf_op jit(solution)/shard_map/ppermute | solution.py:550
  90.7 1.7 %maximum_select_fusion.1 = f32[16,24,128]{2,1,0:T(8,128)} fusion(f32[8,24,128]{2,1,0:T(8,128)S(1)} %collective-permute-done.7, f32[8,24,128]{2,1,0:T(8,128)} %get-tuple-element.23, pred[]{:T(512)S(6)} %eq.4), kind=kLoop, calls=%fused_computation.1 | loop fusion | flops 147456 | bytes 393217 | tf_op jit(solution)/shard_map/jit(_where)/select_n | solution.py:539
  92.4 0.5 collective-permute-done.11
  92.9 0.1 reshape.15
  93.0 0.8 copy.16
  93.8 0.5 slice_bitcast_fusion
  94.4 1.3 %maximum_select_fusion = bf16[16,16,24,128]{3,2,1,0:T(8,128)(2,1)} fusion(bf16[16,8,24,128]{3,2,1,0:T(8,128)(2,1)S(1)} %collective-permute-done.12, bf16[16,8,24,128]{3,2,1,0:T(8,128)(2,1)S(1)} %copy-done.1, pred[]{:T(512)S(6)} %eq.4), kind=kLoop, calls=%fused_computation | loop fusion | flops 2359296 | bytes 3145729 | tf_op jit(solution)/shard_map/jit(_where)/select_n | solution.py:539
  (29 shorter events, 0.6 us)
Async XLA Ops:
  0.6 20.0 %copy-start.6 = (bf16[27,16,16]{0,2,1:T(8,128)(2,1)S(1)}, bf16[27,16,16]{0,2,1:T(8,128)(2,1)}, u32[]{:S(2)}) copy-start(bf16[27,16,16]{0,2,1:T(8,128)(2,1)} %param.6) | copy-start | bytes 41476
  7.0 27.1 %collective-permute-start = (bf16[12,480,128]{2,1,0:T(8,128)(2,1)}, bf16[12,480,128]{2,1,0:T(8,128)(2,1)S(1)}, u32[]{:S(2)}, u32[]{:S(2)}) collective-permute-start(bf16[12,480,128]{2,1,0:T(8,128)(2,1)} %get-tuple-element.19), channel_id=1, source_target_pairs={{0,1},{1,0},{2,3},{3,2},{4,5},{5,4},{6,7},{7,6},{8,9},{9,8},{10,11... | collective-permute-start | bytes 4423688 | tf_op jit(solution)/shard_map/ppermute | solution.py:501
  7.5 11.1 %collective-permute-start.3 = (bf16[16,80,128]{2,1,0:T(8,128)(2,1)}, bf16[16,80,128]{2,1,0:T(8,128)(2,1)S(1)}, u32[]{:S(2)}, u32[]{:S(2)}) collective-permute-start(bf16[16,80,128]{2,1,0:T(8,128)(2,1)} %get-tuple-element.22), channel_id=1, source_target_pairs={{0,2},{1,3},{2,0},{3,1},{4,6},{5,7},{6,4},{7,5},{8,10},{9,11},{10,... | collective-permute-start | bytes 983048 | tf_op jit(solution)/shard_map/ppermute | solution.py:501
  10.0 24.1 %collective-permute-start.1 = (bf16[4,480,128]{2,1,0:T(8,128)(2,1)}, bf16[4,480,128]{2,1,0:T(8,128)(2,1)S(1)}, u32[]{:S(2)}, u32[]{:S(2)}) collective-permute-start(bf16[4,480,128]{2,1,0:T(8,128)(2,1)} %get-tuple-element.20), channel_id=1, source_target_pairs={{0,4},{2,6},{4,8},{5,1},{6,10},{7,3},{8,12},{9,5},{10,14},{11,7},{... | collective-permute-start | bytes 1474568 | tf_op jit(solution)/shard_map/ppermute | solution.py:501
  13.5 20.6 %collective-permute-start.2 = (bf16[4,480,128]{2,1,0:T(8,128)(2,1)}, bf16[4,480,128]{2,1,0:T(8,128)(2,1)S(1)}, u32[]{:S(2)}, u32[]{:S(2)}) collective-permute-start(bf16[4,480,128]{2,1,0:T(8,128)(2,1)} %get-tuple-element.21), channel_id=1, source_target_pairs={{1,4},{3,6},{4,1},{5,8},{6,3},{7,10},{8,5},{9,12},{10,7},{11,14},{... | collective-permute-start | bytes 1474568 | tf_op jit(solution)/shard_map/ppermute | solution.py:501
  18.6 15.6 %copy-start.2 = (bf16[16,80,128]{2,1,0:T(8,128)(2,1)}, bf16[16,80,128]{2,1,0:T(8,128)(2,1)S(1)}, u32[]{:S(2)}) copy-start(bf16[16,80,128]{2,1,0:T(8,128)(2,1)S(1)} %collective-permute-done.3.refs_7_) | copy-start | bytes 983044
  18.6 15.5 %collective-permute-start.4 = (bf16[16,80,128]{2,1,0:T(8,128)(2,1)S(1)}, bf16[16,80,128]{2,1,0:T(8,128)(2,1)S(1)}, u32[]{:S(2)}, u32[]{:S(2)}) collective-permute-start(bf16[16,80,128]{2,1,0:T(8,128)(2,1)S(1)} %collective-permute-done.3.refs_7_), channel_id=1, source_target_pairs={{0,1},{1,0},{2,3},{3,2},{4,5},{5,4},{6,7},{7,6},{8,9},{9,8},{10,11... | collective-permute-start | bytes 983048 | tf_op jit(solution)/shard_map/ppermute | solution.py:501
  19.3 1.9 %collective-permute-start.6 = (bf16[4,80,128]{2,1,0:T(8,128)(2,1)}, bf16[4,80,128]{2,1,0:T(8,128)(2,1)}, u32[]{:S(2)}, u32[]{:S(2)}) collective-permute-start(bf16[4,80,128]{2,1,0:T(8,128)(2,1)} %get-tuple-element.32), channel_id=1, source_target_pairs={{1,4},{3,6},{4,1},{5,8},{6,3},{7,10},{8,5},{9,12},{10,7},{11,14},{... | collective-permute-start | bytes 245768 | tf_op jit(solution)/shard_map/ppermute | solution.py:501
  21.3 12.8 %collective-permute-start.5 = (bf16[4,80,128]{2,1,0:T(8,128)(2,1)S(1)}, bf16[4,80,128]{2,1,0:T(8,128)(2,1)S(1)}, u32[]{:S(2)}, u32[]{:S(2)}) collective-permute-start(bf16[4,80,128]{2,1,0:T(8,128)(2,1)S(1)} %get-tuple-element.33), channel_id=1, source_target_pairs={{0,4},{2,6},{4,8},{5,1},{6,10},{7,3},{8,12},{9,5},{10,14},{11,7},{... | collective-permute-start | bytes 245768 | tf_op jit(solution)/shard_map/ppermute | solution.py:501
  34.1 0.6 copy-start.7
  34.1 0.8 copy-start.3
  34.1 1.0 copy-start.4
  34.1 1.0 %copy-start.5 = (bf16[16,80,128]{2,1,0:T(8,128)(2,1)}, bf16[16,80,128]{2,1,0:T(8,128)(2,1)S(1)}, u32[]{:S(2)}) copy-start(bf16[16,80,128]{2,1,0:T(8,128)(2,1)S(1)} %collective-permute-done.4.refs_8_) | copy-start | bytes 983044
  34.2 1.5 %copy-start = (bf16[12,480,128]{2,1,0:T(8,128)(2,1)}, bf16[12,480,128]{2,1,0:T(8,128)(2,1)S(1)}, u32[]{:S(2)}) copy-start(bf16[12,480,128]{2,1,0:T(8,128)(2,1)S(1)} %collective-permute-done.refs_4_) | copy-start | bytes 4423684
  76.9 17.5 %copy-start.1 = (bf16[16,8,24,128]{3,2,1,0:T(8,128)(2,1)S(1)}, bf16[16,8,24,128]{3,2,1,0:T(8,128)(2,1)}, u32[]{:S(2)}) copy-start(bf16[16,8,24,128]{3,2,1,0:T(8,128)(2,1)} %get-tuple-element.26) | copy-start | bytes 2359300
  76.9 17.5 %collective-permute-start.12 = (bf16[16,8,24,128]{3,2,1,0:T(8,128)(2,1)}, bf16[16,8,24,128]{3,2,1,0:T(8,128)(2,1)S(1)}, u32[]{:S(2)}, u32[]{:S(2)}) collective-permute-start(bf16[16,8,24,128]{3,2,1,0:T(8,128)(2,1)} %get-tuple-element.27), channel_id=1, source_target_pairs={{0,1},{1,0},{2,3},{3,2},{4,5},{5,4},{6,7},{7,6},{8,9},{9,8},{10,11... | collective-permute-start | bytes 2359304 | tf_op jit(solution)/shard_map/ppermute | solution.py:501
  76.9 13.8 %collective-permute-start.7 = (f32[8,24,128]{2,1,0:T(8,128)}, f32[8,24,128]{2,1,0:T(8,128)S(1)}, u32[]{:S(2)}, u32[]{:S(2)}) collective-permute-start(f32[8,24,128]{2,1,0:T(8,128)} %get-tuple-element.24), channel_id=1, source_target_pairs={{0,1},{1,0},{2,3},{3,2},{4,5},{5,4},{6,7},{7,6},{8,9},{9,8},{10,11... | collective-permute-start | bytes 294920 | tf_op jit(solution)/shard_map/ppermute | solution.py:501
  77.4 2.2 %collective-permute-start.8 = (f32[56,128]{1,0:T(8,128)}, f32[56,128]{1,0:T(8,128)S(1)}, u32[]{:S(2)}, u32[]{:S(2)}) collective-permute-start(f32[56,128]{1,0:T(8,128)} %get-tuple-element.25), channel_id=1, source_target_pairs={{0,1},{1,0},{2,3},{3,2},{4,5},{5,4},{6,7},{7,6},{8,9},{9,8},{10,11... | collective-permute-start | bytes 86024 | tf_op jit(solution)/shard_map/ppermute | solution.py:501
  80.4 3.9 %collective-permute-start.9 = (f32[56,128]{1,0:T(8,128)S(1)}, f32[56,128]{1,0:T(8,128)S(1)}, u32[]{:S(2)}, u32[]{:S(2)}) collective-permute-start(f32[56,128]{1,0:T(8,128)S(1)} %add.20), channel_id=1, source_target_pairs={{0,2},{2,0},{1,3},{3,1},{4,6},{6,4},{5,7},{7,5},{8,10},{10,8},{9,1... | collective-permute-start | bytes 86024 | tf_op jit(solution)/shard_map/ppermute | solution.py:550
  84.2 3.9 %collective-permute-start.10 = (f32[56,128]{1,0:T(8,128)S(1)}, f32[56,128]{1,0:T(8,128)S(1)}, u32[]{:S(2)}, u32[]{:S(2)}) collective-permute-start(f32[56,128]{1,0:T(8,128)S(1)} %add.21), channel_id=1, source_target_pairs={{0,4},{4,0},{8,12},{12,8},{1,5},{5,1},{9,13},{13,9},{2,6},{6,2},{1... | collective-permute-start | bytes 86024 | tf_op jit(solution)/shard_map/ppermute | solution.py:550
  88.1 4.8 %collective-permute-start.11 = (f32[56,128]{1,0:T(8,128)S(1)}, f32[56,128]{1,0:T(8,128)S(1)}, u32[]{:S(2)}, u32[]{:S(2)}) collective-permute-start(f32[56,128]{1,0:T(8,128)S(1)} %add.22), channel_id=1, source_target_pairs={{0,8},{4,12},{8,0},{12,4},{1,9},{5,13},{9,1},{13,5},{2,10},{6,14},... | collective-permute-start | bytes 86024 | tf_op jit(solution)/shard_map/ppermute | solution.py:550

commit v2 on v1

--- a/solution.py
+++ b/solution.py
@@ -7,6 +7,7 @@
 
 GROUP = ("gx", "gy", "gz")
 HALO = 4
+STRIP = 3
 F32 = jnp.float32
 BF16 = jnp.bfloat16
 
@@ -81,29 +82,32 @@
         out_shape=[jax.ShapeDtypeStruct(s + (lanes,), BF16) for s in shapes],
         in_specs=[vmem] * 3,
         out_specs=[vmem] * len(shapes),
+        compiler_params=pltpu.CompilerParams(vmem_limit_bytes=14 * 1024 * 1024),
         name="pack",
     )(feats, perm, source)
 
 
-def weights_kernel(base, forward, backward):
-    channels = base.shape[2]
+def weights_kernel(base, flipped, forward, backward):
+    channels = base.shape[1]
     taps = 3 * channels
     block = 8 * channels
-    width = forward.shape[1]
+    width = backward.shape[1]
     size = -(-width // 128) * 128
     blank = jnp.zeros((channels, size - 3 * taps), F32)
     place = lax.broadcasted_iota(jnp.int32, (block, size), 0) % 8
     for dx in range(3):
-        line = jnp.concatenate([base[0, dx].astype(F32), blank], axis=1)
-        for y in range(8):
+        line = jnp.concatenate([base[dx].astype(F32), blank], axis=1)
+        for y in range(STRIP):
             moved = line if y == 0 else pltpu.roll(line, y * taps, 1)
-            start = dx * block + y * channels
-            forward[start : start + channels, :] = moved[:, :width].astype(BF16)
-        line = jnp.concatenate([base[1, dx].astype(F32), blank], axis=1)
+            start = (dx * STRIP + y) * channels
+            forward[start : start + channels, :] = moved[:, : forward.shape[1]].astype(BF16)
+        line = jnp.concatenate([flipped[dx].astype(F32), blank], axis=1)
         lines = jnp.broadcast_to(line[:, None, :], (channels, 8, size)).reshape(block, size)
         out = lines
         for y in range(1, 8):
-            out = jnp.where(place == y, pltpu.roll(lines, y * taps, 1), out)
+            moved = pltpu.roll(line, y * taps, 1)
+            lines = jnp.broadcast_to(moved[:, None, :], (channels, 8, size)).reshape(block, size)
+            out = jnp.where(place == y, lines, out)
         backward[dx * block : (dx + 1) * block, :] = out[:, :width].astype(BF16)
 
 
@@ -113,10 +117,14 @@
     base = grid.transpose(0, 2, 1, 3).reshape(3, channels, 9 * channels)
     flipped = grid[::-1, ::-1].transpose(0, 3, 1, 2).reshape(3, channels, 9 * channels)
     vmem = pl.BlockSpec(memory_space=pltpu.VMEM)
-    shape = jax.ShapeDtypeStruct((24 * channels, 30 * channels), BF16)
+    shapes = [
+        jax.ShapeDtypeStruct((3 * STRIP * channels, 3 * (STRIP + 2) * channels), BF16),
+        jax.ShapeDtypeStruct((24 * channels, 30 * channels), BF16),
+    ]
     return pl.pallas_call(
-        weights_kernel, out_shape=[shape, shape], in_specs=[vmem], out_specs=[vmem, vmem], name="weights"
-    )(jnp.stack([base, flipped]))
+        weights_kernel, out_shape=shapes, in_specs=[vmem] * 2, out_specs=[vmem] * 2,
+        compiler_params=pltpu.CompilerParams(vmem_limit_bytes=8 * 1024 * 1024), name="weights",
+    )(base, flipped)
 
 
 def sigmoid(value):
@@ -127,9 +135,8 @@
     edges = rest[: 4 * sides]
     (
         res_own, res_send, fg_own, fg_send, grads,
-        raw_mine, raw_other, edge_mine, edge_other, sems,
         fwide, slot_a, slot_b, pre_ref, coef, src, vfield, face_x, face_y, face_z, rfield, afield,
-        acc_a, acc_b, kacc, pacc,
+        conv_a, conv_b, acc_a, acc_b, kacc, pacc,
     ) = rest[4 * sides :]
     half = lax.axis_index("gz")
     at_x = lax.axis_index("gx")
@@ -145,66 +152,32 @@
     ext_x = wide + HALO
     inner = ext_x - 2 * HALO
     taps = 3 * channels
-    window = 10 * taps
     block = 8 * channels
     yblocks = ext_y // 8
+    strip = STRIP * channels
+    strips = (ext_y - 2) // STRIP
     oblocks = rows // 8
     cell_rows = rows * channels
     edge_rows = HALO * channels
-
-    most = pl.ds(HALO * (1 - half), wide)
-    side_part = pl.ds(wide * half, HALO)
-    held = pl.ds(HALO * half, wide)
-    moves = [
-        (own.at[held], raw_mine.at[most]),
-        (near, raw_mine.at[side_part]),
-        (swap, raw_other.at[most]),
-        (far, raw_other.at[side_part]),
-    ]
-    for s in range(sides):
-        e_own, e_swap, e_near, e_far = edges[4 * s : 4 * s + 4]
-        moves += [
-            (e_own.at[held], edge_mine.at[s, most]),
-            (e_near, edge_mine.at[s, side_part]),
-            (e_swap.at[held], edge_other.at[s, most]),
-            (e_far, edge_other.at[s, side_part]),
-        ]
-    copies = [pltpu.make_async_copy(a, b, sems.at[k]) for k, (a, b) in enumerate(moves)]
-    for copy in copies:
-        copy.start()
 
     lane_row = lax.broadcasted_iota(jnp.int32, (1, zsize), 1)
     not_first = jnp.where(lane_row == 0, 0.0, 1.0).astype(BF16)
     not_last = jnp.where(lane_row == zsize - 1, 0.0, 1.0).astype(BF16)
     sub = lax.broadcasted_iota(jnp.int32, (channels, zsize), 0)
     proj_rows = jnp.zeros((channels, zsize), F32)
-    tile_lane = lax.broadcasted_iota(jnp.int32, (16, 2 * block), 1) % block
-    tile_row = lax.broadcasted_iota(jnp.int32, (16, 2 * block), 0)
-    tile_low = lax.broadcasted_iota(jnp.int32, (16, 2 * block), 1) < block
-    proj_lanes = jnp.zeros((16, 2 * block), F32)
     for c in range(channels):
         proj_rows = jnp.where(sub == c, proj[c], proj_rows)
-        proj_lanes = jnp.where(tile_lane % channels == c, proj[c], proj_lanes)
     proj_block = jnp.concatenate([proj_rows] * 8, axis=0)
-    proj_hi = proj_lanes.astype(BF16).astype(F32)
-    on_row = tile_lane // channels == tile_row % 8
-    reduce_hi = jnp.where(on_row & (tile_row < 8), proj_hi, 0.0)
-    reduce_lo = jnp.where(on_row & (tile_row >= 8) & tile_low, proj_lanes - proj_hi, 0.0)
-    reducer = (reduce_hi + reduce_lo).astype(BF16)
     row_index = lax.broadcasted_iota(jnp.int32, (ext_y, zsize), 0)
     y_inside = ((row_index >= HALO) | has_ylo) & ((row_index < HALO + rows) | has_yhi)
     lane_index = lax.broadcasted_iota(jnp.int32, (ext_y, zsize), 1)
-    zero = jnp.zeros((1, taps, lanes), BF16)
-    for e in range(ext_x):
-        for s in range(2):
-            fwide[e, s, 0:1] = zero
-            fwide[e, s, ext_y + 1 : ext_y + 2] = zero
+    for px in range(ext_x - 2):
+        pre_ref[px, :channels, :] = jnp.zeros((channels, zsize), F32)
+        pre_ref[px, (ext_y - 1) * channels :, :] = jnp.zeros((channels, zsize), F32)
     kacc[...] = jnp.zeros(kacc.shape, F32)
     pacc[...] = jnp.zeros(pacc.shape, F32)
-    acc_a[...] = jnp.zeros(acc_a.shape, F32)
-    acc_b[...] = jnp.zeros(acc_b.shape, F32)
-    for copy in copies:
-        copy.wait()
+    conv_a[...] = jnp.zeros(conv_a.shape, F32)
+    conv_b[...] = jnp.zeros(conv_b.shape, F32)
 
     def spread(ref, value, y0):
         n = value.shape[0] // channels
@@ -218,11 +191,21 @@
     def joined(mine, other):
         return jnp.concatenate([jnp.where(half == 0, mine, other), jnp.where(half == 0, other, mine)], axis=1)
 
+    def place(e):
+        at = e - HALO * (1 - half)
+        most = (at >= 0) & (at < wide)
+        return most, jnp.clip(at, 0, wide - 1), jnp.clip(e - wide * half, 0, HALO - 1)
+
     def part(e, start, stop):
-        return joined(raw_mine[e, start:stop], raw_other[e, start:stop])
+        most, at, beside = place(e)
+        mine = jnp.where(most, own[at + HALO * half, start:stop], near[beside, start:stop])
+        return joined(mine, jnp.where(most, swap[at, start:stop], far[beside, start:stop]))
 
     def edge_part(s, e, start, stop):
-        return joined(edge_mine[s, e, start:stop], edge_other[s, e, start:stop])
+        e_own, e_swap, e_near, e_far = edges[4 * s : 4 * s + 4]
+        most, at, beside = place(e)
+        mine = jnp.where(most, e_own[at + HALO * half, start:stop], e_near[beside, start:stop])
+        return joined(mine, jnp.where(most, e_swap[at + HALO * half, start:stop], e_far[beside, start:stop]))
 
     def face(a, b):
         return 2.0 * a * b / (a + b)
@@ -237,7 +220,7 @@
             value = jnp.concatenate([jnp.where(has_ylo, edge_part(0, e, 0, edge_rows), blank), value], axis=0)
         if start + 8 > rows:
             value = jnp.concatenate([value, jnp.where(has_yhi, edge_part(sides - 1, e, 0, edge_rows), blank)], axis=0)
-        spread(fwide.at[e], value, 8 * k + 1)
+        spread(fwide.at[e], value, 8 * k)
 
     def fill_fields(e):
         centre = part(e, cell_rows, cell_rows + 4 * rows).astype(F32)
@@ -268,40 +251,44 @@
     def masked(e, value):
         return jnp.where(y_inside & x_inside(e), value, 0.0)
 
-    def taps_of(ref, y0):
-        return jnp.concatenate([ref[s, y0 : y0 + 10].reshape(window, lanes) for s in range(2)], axis=1)
-
-    def convolve(e, yb):
-        result = jnp.dot(weights_fwd[...], taps_of(fwide.at[e], 8 * yb), preferred_element_type=F32)
-        pre_ref[jnp.maximum(e - 2, 0), yb] = acc_b[yb] + result[2 * block :]
-        acc_b[yb] = acc_a[yb] + result[block : 2 * block]
-        acc_a[yb] = result[:block]
+    def taps_of(ref, y0, n):
+        return jnp.concatenate([ref[s, y0 : y0 + n].reshape(n * taps, lanes) for s in range(2)], axis=1)
+
+    def convolve(e, k):
+        result = jnp.dot(
+            weights_fwd[...], taps_of(fwide.at[e], STRIP * k, STRIP + 2), preferred_element_type=F32
+        )
+        start = (1 + STRIP * k) * channels
+        pre_ref[jnp.maximum(e - 2, 0), start : start + strip] = conv_b[k] + result[2 * strip :]
+        conv_b[k] = conv_a[k] + result[strip : 2 * strip]
+        conv_a[k] = result[:strip]
 
     def activate(px, yb):
-        pre = pre_ref[px, yb]
+        pre = pre_ref[px, yb * block : (yb + 1) * block]
         active = pre * sigmoid(pre)
-        high = active.astype(BF16)
-        low = (active - high.astype(F32)).astype(BF16)
-        sums = jnp.dot(reducer, jnp.concatenate([high, low], axis=0), preferred_element_type=F32)
+        sums = jnp.sum((active * proj_block).reshape(8, channels, zsize), axis=1)
         inside = y_inside[8 * yb : 8 * yb + 8] & x_inside(px + 1)
-        vfield[px, 8 * yb : 8 * yb + 8, :] = jnp.where(inside, sums[:8] + sums[8:], 0.0)
+        vfield[px, 8 * yb : 8 * yb + 8, :] = jnp.where(inside, sums, 0.0)
 
     for k in range(yblocks):
         fill_cells(0, k)
     fill_fields(0)
 
     def conv_step(e, carry):
-        for k in range(yblocks):
-            activate(jnp.maximum(e - 4, 0), k)
+        for k in range(strips):
             convolve(e - 1, k)
-            fill_cells(e, k)
+            for m in range(yblocks):
+                if m * strips // yblocks == k:
+                    activate(jnp.maximum(e - 4, 0), m)
+                    fill_cells(e, m)
         fill_fields(e)
         return carry
 
     lax.fori_loop(1, ext_x, conv_step, 0)
+    for k in range(strips):
+        convolve(ext_x - 1, k)
     for k in range(yblocks):
         activate(ext_x - 4, k)
-        convolve(ext_x - 1, k)
     for k in range(yblocks):
         activate(ext_x - 3, k)
 
@@ -345,12 +332,12 @@
     lax.fori_loop(0, inner, residual_out, 0, unroll=4)
 
     def grad_block(i, yb, slot):
-        pre = pre_ref[i + 2, yb]
+        pre = pre_ref[i + 2, yb * block : (yb + 1) * block]
         sig = sigmoid(pre)
         near_adj = afield[i, 8 * yb : 8 * yb + 8, :]
         adj = jnp.broadcast_to(near_adj[:, None, :], (8, channels, zsize)).reshape(block, zsize)
         slope = sig * (1.0 + pre * (1.0 - sig))
-        spread(slot, (adj * proj_block * slope).astype(BF16), 8 * yb + 1)
+        spread(slot, (adj * proj_block * slope).astype(BF16), 8 * yb)
         lo = max(HALO - 8 * yb, 0)
         hi = min(HALO + rows - 8 * yb, 8)
         term = (adj * (pre * sig))[lo * channels : hi * channels]
@@ -360,7 +347,7 @@
         pacc[...] += jnp.where((i >= 1) & (i <= inner), total, 0.0)
 
     def back_product(b, slot, weights):
-        return jnp.dot(weights, taps_of(slot, HALO + 8 * b), preferred_element_type=F32)
+        return jnp.dot(weights, taps_of(slot, HALO - 1 + 8 * b, 10), preferred_element_type=F32)
 
     def store_plane(x, parts):
         value = jnp.concatenate([p.reshape(channels, 8, zsize) for p in parts], axis=1).astype(BF16)
@@ -373,7 +360,7 @@
         parts = []
         centres = []
         for b in range(oblocks):
-            y0 = HALO + 1 + 8 * b
+            y0 = HALO + 8 * b
             pieces = [slot[s, y0 : y0 + 8, channels : 2 * channels, :].reshape(block, lanes) for s in range(2)]
             centres.append(jnp.concatenate(pieces, axis=1))
         for k in range(max(3, oblocks, yblocks)):
@@ -386,7 +373,7 @@
                 total = kacc[k]
                 for b in range(oblocks):
                     total = total + lax.dot_general(
-                        taps_of(fwide.at[i + HALO - 2 + k], HALO + 8 * b),
+                        taps_of(fwide.at[i + HALO - 2 + k], HALO - 1 + 8 * b, 10),
                         centres[b],
                         (((1,), (1,)), ((), ())),
                         preferred_element_type=F32,
@@ -448,9 +435,9 @@
     grad_rows = 27 * channels * channels // block
     out_rows = -(-(grad_rows + 1) // 8) * 8
     vmem = pl.BlockSpec(memory_space=pltpu.VMEM)
-    anywhere = pl.BlockSpec(memory_space=pl.ANY)
     plane = (ext_y, zsize)
-    slot = pltpu.VMEM((2, ext_y + 2, taps, lanes), BF16)
+    slot = pltpu.VMEM((2, ext_y, taps, lanes), BF16)
+    strip = pltpu.VMEM(((ext_y - 2) // STRIP, STRIP * channels, zsize), F32)
     return pl.pallas_call(
         lambda *refs: main_kernel(channels, rows, sides, *refs),
         out_shape=[
@@ -460,18 +447,13 @@
             jax.ShapeDtypeStruct((channels, inner, rows, lanes), BF16),
             jax.ShapeDtypeStruct((out_rows, block), F32),
         ],
-        in_specs=[pl.BlockSpec(memory_space=pltpu.SMEM)] + [vmem] * 2 + [anywhere] * (len(tensors) + len(edges)),
+        in_specs=[pl.BlockSpec(memory_space=pltpu.SMEM)] + [vmem] * (2 + len(tensors) + len(edges)),
         out_specs=[vmem] * 5,
         scratch_shapes=[
-            pltpu.VMEM((ext_x,) + own.shape[1:], BF16),
-            pltpu.VMEM((ext_x,) + own.shape[1:], BF16),
-            pltpu.VMEM((sides, ext_x) + edges[0].shape[1:], BF16),
-            pltpu.VMEM((sides, ext_x) + edges[0].shape[1:], BF16),
-            pltpu.SemaphoreType.DMA((4 + 4 * sides,)),
-            pltpu.VMEM((ext_x, 2, ext_y + 2, taps, lanes), BF16),
+            pltpu.VMEM((ext_x, 2, ext_y, taps, lanes), BF16),
             slot,
             slot,
-            pltpu.VMEM((ext_x - 2, yblocks, block, zsize), F32),
+            pltpu.VMEM((ext_x - 2, ext_y * channels, zsize), F32),
             pltpu.VMEM((ext_x,) + plane, F32),
             pltpu.VMEM((ext_x,) + plane, F32),
             pltpu.VMEM((ext_x - 2,) + plane, F32),
@@ -480,12 +462,14 @@
             pltpu.VMEM((ext_x,) + plane, F32),
             pltpu.VMEM((ext_x - 4,) + plane, F32),
             pltpu.VMEM((ext_x - 6,) + plane, F32),
-            pltpu.VMEM((yblocks, block, zsize), F32),
-            pltpu.VMEM((yblocks, block, zsize), F32),
+            strip,
+            strip,
+            pltpu.VMEM((rows // 8, block, zsize), F32),
+            pltpu.VMEM((rows // 8, block, zsize), F32),
             pltpu.VMEM((3, 10 * taps, block), F32),
             pltpu.VMEM((channels, zsize), F32),
         ],
-        compiler_params=pltpu.CompilerParams(vmem_limit_bytes=58 * 1024 * 1024),
+        compiler_params=pltpu.CompilerParams(vmem_limit_bytes=40 * 1024 * 1024),
         name="step",
     )(proj, *weights, *tensors, *edges)
 
@@ -519,7 +503,9 @@
             return y + 1 if side == 0 else y - 1
 
         received.append(send(edges[side], lambda x, y, z: (x, step_y(y), z)))
-    tensors = [own, partner(swap), to_near(near), to_far(far)]
+    swapped = partner(swap)
+    *received, swapped = lax.optimization_barrier((*received, swapped))
+    tensors = [own, swapped, to_near(near), to_far(far)]
     wide = planes - HALO
     got = []
     for value in received:

time: 96.1 us -> 76.1 us (0.79)
  Pallas kernels: 50.4 us -> 27.9 us
  local copies, waits for them, and re-layouts: 4.31 us -> 12.4 us
  other arithmetic: 4.35 us -> 2 us
  starting transfers between devices: 23.2 us -> 20.9 us
  waiting for transfers between devices: 12.6 us -> 11.6 us
    pallas_call x1, Pallas kernels: 41.2 us -> 23.5 us  [main(): pl.pallas_call(lambda *refs: main_kernel(channels, rows, sides, *refs), o...]
    unnamed x18 -> x16, local copies, waits for them, and re-layouts: 2.53 us -> 5.82 us
    pallas_call x1, Pallas kernels: 6.4 us -> 3.61 us  [pack(): pl.pallas_call(lambda *refs: pack_kernel(sides, *refs), out_shape=[jax.Sh...]
    ppermute x10, starting transfers between devices: 18.5 us -> 15.8 us  [send(): return lax.ppermute(value, GROUP, routes(sizes, target))]
    reshape x0 -> x2, local copies, waits for them, and re-layouts: none -> 1.98 us  [the longest x1 0.99 us: banded_weights(): base = grid.transpose(0, 2, 1, 3).reshape(3, channels, 9 * channels)]
    pallas_call x1, Pallas kernels: 2.8 us -> 0.85 us  [banded_weights(): pl.pallas_call(weights_kernel, out_shape=shapes, in_specs=[vmem] * 2, out...]
    ppermute x10, waiting for transfers between devices: 6.49 us -> 4.95 us  [send(): return lax.ppermute(value, GROUP, routes(sizes, target))]
    rev x1, local copies, waits for them, and re-layouts: 0.02 us -> 1.56 us  [banded_weights(): grid[::-1, ::-1].transpose(0, 3, 1, 2).reshape(3, channels, 9 * channels)]
  transfers between devices with their start and end apart: 13 -> 13, of which waited for: 5 -> 5; matrix products, arithmetic and copies ran while one was open for 6% -> 12% of each run, Pallas kernels for 3% -> 1%
where the time goes in v2:
time: 76.1 us; the launch traced here: 75.7 us
  Pallas kernels  27.9 us (37%)
  starting transfers between devices  20.9 us (27%)
  local copies, waits for them, and re-layouts  12.4 us (16%)
  waiting for transfers between devices  11.6 us (15%)
  other arithmetic  2 us (3%)
    pallas_call x1, Pallas kernels, main(): pl.pallas_call(lambda *refs: main_kernel(channels, rows, sides, *refs), o...  23.5 us
    ppermute x10, starting transfers between devices, send(): return lax.ppermute(value, GROUP, routes(sizes, target))  15.8 us
    ppermute x3, waiting for transfers between devices, local(): lax.ppermute(grads, axis, [(i, i ^ step) for i in range(count)])  6.68 us
    unnamed x16, local copies, waits for them, and re-layouts  5.82 us
    ppermute x3, starting transfers between devices, local(): lax.ppermute(grads, axis, [(i, i ^ step) for i in range(count)])  5.14 us
    ppermute x10, waiting for transfers between devices, send(): return lax.ppermute(value, GROUP, routes(sizes, target))  4.95 us
    pallas_call x1, Pallas kernels, pack(): pl.pallas_call(lambda *refs: pack_kernel(sides, *refs), out_shape=[jax.Sh...  3.61 us
    select_n x2, other arithmetic, ordered(): jnp.where(half == 0, jnp.concatenate([mine, other], axis), jnp.concatenat...  1.98 us
  transfers between devices with their start and end apart: 13, of which 5 were waited for; matrix products, arithmetic and copies ran while one was open for 12% of the time, Pallas kernels for 1%

profile of v2, /device:TPU:0, one launch (start us, length us, event | category | flops | bytes accessed | tf_op | source)
XLA Modules:
  0.0 75.7 jit_solution(9414026382436764824)
XLA Ops:
  0.6 1.4 %copy-done = bf16[16,16,24,128]{3,2,1,0:T(8,128)(2,1)S(1)} copy-done((bf16[16,16,24,128]{3,2,1,0:T(8,128)(2,1)S(1)}, bf16[16,16,24,128]{3,2,1,0:T(8,128)(2,1)}, u32[]{:S(2)}) %copy-start) | copy-done | bytes 1572888
  2.0 0.9 %copy-done.3 = f32[16,24,128]{2,1,0:T(8,128)S(1)} copy-done((f32[16,24,128]{2,1,0:T(8,128)S(1)}, f32[16,24,128]{2,1,0:T(8,128)}, u32[]{:S(2)}) %copy-start.3) | copy-done | bytes 196632
  3.0 0.9 %copy-done.4 = f32[16,24,128]{2,1,0:T(8,128)S(1)} copy-done((f32[16,24,128]{2,1,0:T(8,128)S(1)}, f32[16,24,128]{2,1,0:T(8,128)}, u32[]{:S(2)}) %copy-start.4) | copy-done | bytes 196632
  3.9 3.6 %pack.1 = (bf16[16,480,128]{2,1,0:T(8,128)(2,1)S(1)}, bf16[12,480,128]{2,1,0:T(8,128)(2,1)S(1)}, bf16[4,480,128]{2,1,0:T(8,128)(2,1)}, bf16[4,480,128]{2,1,0:T(8,128)(2,1)}, bf16[16,80,128]{2,1,0:T(8,128)(2,1)S(1)}) custom-call(bf16[16,16,24,128]{3,2,1,0:T(8,128)(2,1)S(1)} %copy-done, f32[16,24,128]{2,1,0:T(8,128)S(1)} %copy-done.3, f32[16,24,128]{2,1,0:T(8,128)S(1)} %copy-done.4), custom_call_target="tpu_custom_call" | custom-call | tf_op jit(solution)/shard_map/pack/pallas_call | solution.py:80
  7.5 0.5 collective-permute-start.1
  8.0 2.5 %collective-permute-start = (bf16[16,80,128]{2,1,0:T(8,128)(2,1)S(1)}, bf16[16,80,128]{2,1,0:T(8,128)(2,1)}, u32[]{:S(2)}, u32[]{:S(2)}) collective-permute-start(bf16[16,80,128]{2,1,0:T(8,128)(2,1)S(1)} %get-tuple-element.21), channel_id=1, source_target_pairs={{0,2},{1,3},{2,0},{3,1},{4,6},{5,7},{6,4},{7,5},{8,10},{9,11},{10,... | collective-permute-start | bytes 983048 | tf_op jit(solution)/shard_map/ppermute | solution.py:485
  10.5 4.3 %collective-permute-start.2 = (bf16[4,480,128]{2,1,0:T(8,128)(2,1)}, bf16[4,480,128]{2,1,0:T(8,128)(2,1)}, u32[]{:S(2)}, u32[]{:S(2)}) collective-permute-start(bf16[4,480,128]{2,1,0:T(8,128)(2,1)} %get-tuple-element.24), channel_id=1, source_target_pairs={{0,4},{2,6},{4,8},{5,1},{6,10},{7,3},{8,12},{9,5},{10,14},{11,7},{... | collective-permute-start | bytes 1474568 | tf_op jit(solution)/shard_map/ppermute | solution.py:485
  14.8 1.4 %collective-permute-start.3 = (bf16[4,480,128]{2,1,0:T(8,128)(2,1)}, bf16[4,480,128]{2,1,0:T(8,128)(2,1)}, u32[]{:S(2)}, u32[]{:S(2)}) collective-permute-start(bf16[4,480,128]{2,1,0:T(8,128)(2,1)} %get-tuple-element.25), channel_id=1, source_target_pairs={{1,4},{3,6},{4,1},{5,8},{6,3},{7,10},{8,5},{9,12},{10,7},{11,14},{... | collective-permute-start | bytes 1474568 | tf_op jit(solution)/shard_map/ppermute | solution.py:485
  16.2 2.8 %collective-permute-done.refs_7_ = bf16[16,80,128]{2,1,0:T(8,128)(2,1)} collective-permute-done((bf16[16,80,128]{2,1,0:T(8,128)(2,1)S(1)}, bf16[16,80,128]{2,1,0:T(8,128)(2,1)}, u32[]{:S(2)}, u32[]{:S(2)}) %collective-permute-start) | collective-permute-done | bytes 327712 | tf_op jit(solution)/shard_map/ppermute | solution.py:485
  19.0 1.6 %constant_dynamic-slice_fusion = (bf16[4,80,128]{2,1,0:T(8,128)(2,1)}, bf16[4,80,128]{2,1,0:T(8,128)(2,1)}) fusion(bf16[16,80,128]{2,1,0:T(8,128)(2,1)} %collective-permute-done.refs_7_, s32[]{:T(128)S(6)} %select_n.24, s32[]{:T(128)S(6)} %select_n.23), kind=kLoop, calls=%fused_computation.3 | loop fusion | bytes 327688 | tf_op jit(solution)/shard_map/dynamic_slice | solution.py:516
  20.6 1.3 %collective-permute-start.6 = (bf16[4,80,128]{2,1,0:T(8,128)(2,1)}, bf16[4,80,128]{2,1,0:T(8,128)(2,1)}, u32[]{:S(2)}, u32[]{:S(2)}) collective-permute-start(bf16[4,80,128]{2,1,0:T(8,128)(2,1)} %get-tuple-element.36), channel_id=1, source_target_pairs={{1,4},{3,6},{4,1},{5,8},{6,3},{7,10},{8,5},{9,12},{10,7},{11,14},{... | collective-permute-start | bytes 245768 | tf_op jit(solution)/shard_map/ppermute | solution.py:485
  21.9 5.3 %collective-permute-start.5 = (bf16[4,80,128]{2,1,0:T(8,128)(2,1)}, bf16[4,80,128]{2,1,0:T(8,128)(2,1)}, u32[]{:S(2)}, u32[]{:S(2)}) collective-permute-start(bf16[4,80,128]{2,1,0:T(8,128)(2,1)} %get-tuple-element.37), channel_id=1, source_target_pairs={{0,4},{2,6},{4,8},{5,1},{6,10},{7,3},{8,12},{9,5},{10,14},{11,7},{... | collective-permute-start | bytes 245768 | tf_op jit(solution)/shard_map/ppermute | solution.py:485
  27.2 0.8 %copy.17 = bf16[27,16,16]{1,2,0:T(8,128)(2,1)} copy(bf16[27,16,16]{0,2,1:T(8,128)(2,1)S(1)} %copy-done.6) | data formatting | bytes 27648 | tf_op jit(solution)/shard_map/transpose | solution.py:117
  28.0 0.8 %copy.12 = bf16[27,16,16]{2,1,0:T(8,128)(2,1)} copy(bf16[27,16,16]{0,2,1:T(8,128)(2,1)S(1)} %copy-done.6) | data formatting | bytes 27648 | tf_op args[1]
  28.9 1.0 %copy.14.base = bf16[3,16,144]{2,1,0:T(8,128)(2,1)S(1)} copy(bf16[3,16,144]{1,2,0:T(8,128)(2,1)} %bitcast.15) | data formatting | bytes 27648 | tf_op jit(solution)/shard_map/reshape | solution.py:117
  29.9 1.6 %rev.3 = bf16[3,9,16,16]{3,2,1,0:T(8,128)(2,1)} reverse(bf16[3,9,16,16]{3,2,1,0:T(8,128)(2,1)} %bitcast.13), dimensions={0,1} | reverse | bytes 27648 | tf_op jit(solution)/shard_map/rev | solution.py:118
  31.4 1.0 %copy.15.flipped = bf16[3,16,144]{2,1,0:T(8,128)(2,1)S(1)} copy(bf16[3,16,144]{1,2,0:T(8,128)(2,1)} %bitcast.14) | data formatting | bytes 27648 | tf_op jit(solution)/shard_map/reshape | solution.py:118
  32.4 0.9 %weights.1 = (bf16[144,240]{1,0:T(8,128)(2,1)S(1)}, bf16[384,480]{1,0:T(8,128)(2,1)S(1)}) custom-call(bf16[3,16,144]{2,1,0:T(8,128)(2,1)S(1)} %copy.14.base, bf16[3,16,144]{2,1,0:T(8,128)(2,1)S(1)} %copy.15.flipped), custom_call_target="tpu_custom_call" | custom-call | tf_op jit(solution)/shard_map/weights/pallas_call | solution.py:124
  33.3 23.5 %step.1 = (f32[8,24,128]{2,1,0:T(8,128)S(1)}, f32[8,24,128]{2,1,0:T(8,128)}, bf16[16,8,24,128]{3,2,1,0:T(8,128)(2,1)S(1)}, bf16[16,8,24,128]{3,2,1,0:T(8,128)(2,1)}, f32[56,128]{1,0:T(8,128)S(1)}) custom-call(f32[16]{0:T(128)S(1)} %copy-done.5, bf16[144,240]{1,0:T(8,128)(2,1)S(1)} %get-tuple-element.18.refs_1_, ...), custom_call_target="tpu_custom_call" | custom-call | tf_op jit(solution)/shard_map/step/pallas_call | solution.py:441
  56.8 0.9 %copy-done.1 = bf16[16,8,24,128]{3,2,1,0:T(8,128)(2,1)} copy-done((bf16[16,8,24,128]{3,2,1,0:T(8,128)(2,1)}, bf16[16,8,24,128]{3,2,1,0:T(8,128)(2,1)S(1)}, u32[]{:S(2)}) %copy-start.1) | copy-done | bytes 786456
  57.7 0.5 collective-permute-start.7
  58.2 2.2 %collective-permute-done.8 = f32[56,128]{1,0:T(8,128)S(1)} collective-permute-done((f32[56,128]{1,0:T(8,128)S(1)}, f32[56,128]{1,0:T(8,128)S(1)}, u32[]{:S(2)}, u32[]{:S(2)}) %collective-permute-start.8) | collective-permute-done | bytes 28704 | tf_op jit(solution)/shard_map/ppermute | solution.py:485
  60.4 1.7 %collective-permute-start.9 = (f32[56,128]{1,0:T(8,128)S(1)}, f32[56,128]{1,0:T(8,128)S(1)}, u32[]{:S(2)}, u32[]{:S(2)}) collective-permute-start(f32[56,128]{1,0:T(8,128)S(1)} %add.20), channel_id=1, source_target_pairs={{0,2},{2,0},{1,3},{3,1},{4,6},{6,4},{5,7},{7,5},{8,10},{10,8},{9,1... | collective-permute-start | bytes 86024 | tf_op jit(solution)/shard_map/ppermute | solution.py:536
  62.1 2.1 %collective-permute-done.9 = f32[56,128]{1,0:T(8,128)S(1)} collective-permute-done((f32[56,128]{1,0:T(8,128)S(1)}, f32[56,128]{1,0:T(8,128)S(1)}, u32[]{:S(2)}, u32[]{:S(2)}) %collective-permute-start.9) | collective-permute-done | bytes 28704 | tf_op jit(solution)/shard_map/ppermute | solution.py:536
  64.3 1.2 %collective-permute-start.10 = (f32[56,128]{1,0:T(8,128)S(1)}, f32[56,128]{1,0:T(8,128)S(1)}, u32[]{:S(2)}, u32[]{:S(2)}) collective-permute-start(f32[56,128]{1,0:T(8,128)S(1)} %add.21), channel_id=1, source_target_pairs={{0,4},{4,0},{8,12},{12,8},{1,5},{5,1},{9,13},{13,9},{2,6},{6,2},{1... | collective-permute-start | bytes 86024 | tf_op jit(solution)/shard_map/ppermute | solution.py:536
  65.4 2.7 %collective-permute-done.10 = f32[56,128]{1,0:T(8,128)S(1)} collective-permute-done((f32[56,128]{1,0:T(8,128)S(1)}, f32[56,128]{1,0:T(8,128)S(1)}, u32[]{:S(2)}, u32[]{:S(2)}) %collective-permute-start.10) | collective-permute-done | bytes 28704 | tf_op jit(solution)/shard_map/ppermute | solution.py:536
  68.1 2.2 %collective-permute-start.11 = (f32[56,128]{1,0:T(8,128)S(1)}, f32[56,128]{1,0:T(8,128)S(1)}, u32[]{:S(2)}, u32[]{:S(2)}) collective-permute-start(f32[56,128]{1,0:T(8,128)S(1)} %add.22), channel_id=1, source_target_pairs={{0,8},{4,12},{8,0},{12,4},{1,9},{5,13},{9,1},{13,5},{2,10},{6,14},... | collective-permute-start | bytes 86024 | tf_op jit(solution)/shard_map/ppermute | solution.py:536
  70.3 0.7 maximum_select_fusion.1
  71.0 1.9 %collective-permute-done.11 = f32[56,128]{1,0:T(8,128)S(1)} collective-permute-done((f32[56,128]{1,0:T(8,128)S(1)}, f32[56,128]{1,0:T(8,128)S(1)}, u32[]{:S(2)}, u32[]{:S(2)}) %collective-permute-start.11) | collective-permute-done | bytes 28704 | tf_op jit(solution)/shard_map/ppermute | solution.py:536
  73.0 0.8 %copy.16 = f32[27,16,16]{0,2,1:T(8,128)} copy(f32[27,16,16]{1,2,0:T(8,128)S(1)} %bitcast.12) | data formatting | bytes 55296
  73.9 0.5 slice_bitcast_fusion
  74.4 1.3 %maximum_select_fusion = bf16[16,16,24,128]{3,2,1,0:T(8,128)(2,1)} fusion(bf16[16,8,24,128]{3,2,1,0:T(8,128)(2,1)S(1)} %collective-permute-done.12, bf16[16,8,24,128]{3,2,1,0:T(8,128)(2,1)S(1)} %copy-done.2, pred[]{:T(512)S(6)} %eq.4), kind=kLoop, calls=%fused_computation | loop fusion | flops 2359296 | bytes 3145729 | tf_op jit(solution)/shard_map/jit(_where)/select_n | solution.py:525
  (26 shorter events, 0.2 us)
Async XLA Ops:
  0.6 1.4 %copy-start = (bf16[16,16,24,128]{3,2,1,0:T(8,128)(2,1)S(1)}, bf16[16,16,24,128]{3,2,1,0:T(8,128)(2,1)}, u32[]{:S(2)}) copy-start(bf16[16,16,24,128]{3,2,1,0:T(8,128)(2,1)} %refs_0_.2) | copy-start | bytes 4718596
  2.0 0.9 %copy-start.3 = (f32[16,24,128]{2,1,0:T(8,128)S(1)}, f32[16,24,128]{2,1,0:T(8,128)}, u32[]{:S(2)}) copy-start(f32[16,24,128]{2,1,0:T(8,128)} %refs_1_.1) | copy-start | bytes 589828
  3.0 0.9 %copy-start.4 = (f32[16,24,128]{2,1,0:T(8,128)S(1)}, f32[16,24,128]{2,1,0:T(8,128)}, u32[]{:S(2)}) copy-start(f32[16,24,128]{2,1,0:T(8,128)} %refs_2_.1) | copy-start | bytes 589828
  3.9 23.3 %copy-start.6 = (bf16[27,16,16]{0,2,1:T(8,128)(2,1)S(1)}, bf16[27,16,16]{0,2,1:T(8,128)(2,1)}, u32[]{:S(2)}) copy-start(bf16[27,16,16]{0,2,1:T(8,128)(2,1)} %param.6) | copy-start | bytes 41476
  3.9 29.4 %copy-start.5 = (f32[16]{0:T(128)S(1)}, f32[16]{0:T(128)}, u32[]{:S(2)}) copy-start(f32[16]{0:T(128)} %refs_0_.3) | copy-start | bytes 196
  7.5 11.5 %collective-permute-start.1 = (bf16[12,480,128]{2,1,0:T(8,128)(2,1)S(1)}, bf16[12,480,128]{2,1,0:T(8,128)(2,1)S(1)}, u32[]{:S(2)}, u32[]{:S(2)}) collective-permute-start(bf16[12,480,128]{2,1,0:T(8,128)(2,1)S(1)} %get-tuple-element.22), channel_id=1, source_target_pairs={{0,1},{1,0},{2,3},{3,2},{4,5},{5,4},{6,7},{7,6},{8,9},{9,8},{10,11... | collective-permute-start | bytes 4423688 | tf_op jit(solution)/shard_map/ppermute | solution.py:485
  8.0 11.0 %collective-permute-start = (bf16[16,80,128]{2,1,0:T(8,128)(2,1)S(1)}, bf16[16,80,128]{2,1,0:T(8,128)(2,1)}, u32[]{:S(2)}, u32[]{:S(2)}) collective-permute-start(bf16[16,80,128]{2,1,0:T(8,128)(2,1)S(1)} %get-tuple-element.21), channel_id=1, source_target_pairs={{0,2},{1,3},{2,0},{3,1},{4,6},{5,7},{6,4},{7,5},{8,10},{9,11},{10,... | collective-permute-start | bytes 983048 | tf_op jit(solution)/shard_map/ppermute | solution.py:485
  10.5 22.8 %collective-permute-start.2 = (bf16[4,480,128]{2,1,0:T(8,128)(2,1)}, bf16[4,480,128]{2,1,0:T(8,128)(2,1)}, u32[]{:S(2)}, u32[]{:S(2)}) collective-permute-start(bf16[4,480,128]{2,1,0:T(8,128)(2,1)} %get-tuple-element.24), channel_id=1, source_target_pairs={{0,4},{2,6},{4,8},{5,1},{6,10},{7,3},{8,12},{9,5},{10,14},{11,7},{... | collective-permute-start | bytes 1474568 | tf_op jit(solution)/shard_map/ppermute | solution.py:485
  14.8 18.5 %collective-permute-start.3 = (bf16[4,480,128]{2,1,0:T(8,128)(2,1)}, bf16[4,480,128]{2,1,0:T(8,128)(2,1)}, u32[]{:S(2)}, u32[]{:S(2)}) collective-permute-start(bf16[4,480,128]{2,1,0:T(8,128)(2,1)} %get-tuple-element.25), channel_id=1, source_target_pairs={{1,4},{3,6},{4,1},{5,8},{6,3},{7,10},{8,5},{9,12},{10,7},{11,14},{... | collective-permute-start | bytes 1474568 | tf_op jit(solution)/shard_map/ppermute | solution.py:485
  19.0 14.3 %collective-permute-start.4 = (bf16[16,80,128]{2,1,0:T(8,128)(2,1)}, bf16[16,80,128]{2,1,0:T(8,128)(2,1)}, u32[]{:S(2)}, u32[]{:S(2)}) collective-permute-start(bf16[16,80,128]{2,1,0:T(8,128)(2,1)} %collective-permute-done.refs_7_), channel_id=1, source_target_pairs={{0,1},{1,0},{2,3},{3,2},{4,5},{5,4},{6,7},{7,6},{8,9},{9,8},{10,11... | collective-permute-start | bytes 983048 | tf_op jit(solution)/shard_map/ppermute | solution.py:485
  20.6 12.7 %collective-permute-start.6 = (bf16[4,80,128]{2,1,0:T(8,128)(2,1)}, bf16[4,80,128]{2,1,0:T(8,128)(2,1)}, u32[]{:S(2)}, u32[]{:S(2)}) collective-permute-start(bf16[4,80,128]{2,1,0:T(8,128)(2,1)} %get-tuple-element.36), channel_id=1, source_target_pairs={{1,4},{3,6},{4,1},{5,8},{6,3},{7,10},{8,5},{9,12},{10,7},{11,14},{... | collective-permute-start | bytes 245768 | tf_op jit(solution)/shard_map/ppermute | solution.py:485
  21.9 11.5 %collective-permute-start.5 = (bf16[4,80,128]{2,1,0:T(8,128)(2,1)}, bf16[4,80,128]{2,1,0:T(8,128)(2,1)}, u32[]{:S(2)}, u32[]{:S(2)}) collective-permute-start(bf16[4,80,128]{2,1,0:T(8,128)(2,1)} %get-tuple-element.37), channel_id=1, source_target_pairs={{0,4},{2,6},{4,8},{5,1},{6,10},{7,3},{8,12},{9,5},{10,14},{11,7},{... | collective-permute-start | bytes 245768 | tf_op jit(solution)/shard_map/ppermute | solution.py:485
  56.8 0.9 %copy-start.1 = (bf16[16,8,24,128]{3,2,1,0:T(8,128)(2,1)}, bf16[16,8,24,128]{3,2,1,0:T(8,128)(2,1)S(1)}, u32[]{:S(2)}) copy-start(bf16[16,8,24,128]{3,2,1,0:T(8,128)(2,1)S(1)} %get-tuple-element.30) | copy-start | bytes 2359300
  57.7 16.7 %copy-start.2 = (bf16[16,8,24,128]{3,2,1,0:T(8,128)(2,1)S(1)}, bf16[16,8,24,128]{3,2,1,0:T(8,128)(2,1)}, u32[]{:S(2)}) copy-start(bf16[16,8,24,128]{3,2,1,0:T(8,128)(2,1)} %copy-done.1) | copy-start | bytes 2359300
  57.7 16.7 %collective-permute-start.12 = (bf16[16,8,24,128]{3,2,1,0:T(8,128)(2,1)}, bf16[16,8,24,128]{3,2,1,0:T(8,128)(2,1)S(1)}, u32[]{:S(2)}, u32[]{:S(2)}) collective-permute-start(bf16[16,8,24,128]{3,2,1,0:T(8,128)(2,1)} %get-tuple-element.31), channel_id=1, source_target_pairs={{0,1},{1,0},{2,3},{3,2},{4,5},{5,4},{6,7},{7,6},{8,9},{9,8},{10,11... | collective-permute-start | bytes 2359304 | tf_op jit(solution)/shard_map/ppermute | solution.py:485
  57.7 12.6 %collective-permute-start.7 = (f32[8,24,128]{2,1,0:T(8,128)}, f32[8,24,128]{2,1,0:T(8,128)S(1)}, u32[]{:S(2)}, u32[]{:S(2)}) collective-permute-start(f32[8,24,128]{2,1,0:T(8,128)} %get-tuple-element.28), channel_id=1, source_target_pairs={{0,1},{1,0},{2,3},{3,2},{4,5},{5,4},{6,7},{7,6},{8,9},{9,8},{10,11... | collective-permute-start | bytes 294920 | tf_op jit(solution)/shard_map/ppermute | solution.py:485
  58.2 2.2 %collective-permute-start.8 = (f32[56,128]{1,0:T(8,128)S(1)}, f32[56,128]{1,0:T(8,128)S(1)}, u32[]{:S(2)}, u32[]{:S(2)}) collective-permute-start(f32[56,128]{1,0:T(8,128)S(1)} %get-tuple-element.29), channel_id=1, source_target_pairs={{0,1},{1,0},{2,3},{3,2},{4,5},{5,4},{6,7},{7,6},{8,9},{9,8},{10,11... | collective-permute-start | bytes 86024 | tf_op jit(solution)/shard_map/ppermute | solution.py:485
  60.4 3.9 %collective-permute-start.9 = (f32[56,128]{1,0:T(8,128)S(1)}, f32[56,128]{1,0:T(8,128)S(1)}, u32[]{:S(2)}, u32[]{:S(2)}) collective-permute-start(f32[56,128]{1,0:T(8,128)S(1)} %add.20), channel_id=1, source_target_pairs={{0,2},{2,0},{1,3},{3,1},{4,6},{6,4},{5,7},{7,5},{8,10},{10,8},{9,1... | collective-permute-start | bytes 86024 | tf_op jit(solution)/shard_map/ppermute | solution.py:536
  64.3 3.9 %collective-permute-start.10 = (f32[56,128]{1,0:T(8,128)S(1)}, f32[56,128]{1,0:T(8,128)S(1)}, u32[]{:S(2)}, u32[]{:S(2)}) collective-permute-start(f32[56,128]{1,0:T(8,128)S(1)} %add.21), channel_id=1, source_target_pairs={{0,4},{4,0},{8,12},{12,8},{1,5},{5,1},{9,13},{13,9},{2,6},{6,2},{1... | collective-permute-start | bytes 86024 | tf_op jit(solution)/shard_map/ppermute | solution.py:536
  68.1 4.8 %collective-permute-start.11 = (f32[56,128]{1,0:T(8,128)S(1)}, f32[56,128]{1,0:T(8,128)S(1)}, u32[]{:S(2)}, u32[]{:S(2)}) collective-permute-start(f32[56,128]{1,0:T(8,128)S(1)} %add.22), channel_id=1, source_target_pairs={{0,8},{4,12},{8,0},{12,4},{1,9},{5,13},{9,1},{13,5},{2,10},{6,14},... | collective-permute-start | bytes 86024 | tf_op jit(solution)/shard_map/ppermute | solution.py:536
